TPU v7x, 256 devices: a whole 4x4x8 slice. The times are simulated.
256 devices in a mesh: obj: 32 (over z, x), view: 8 (over y, core).
Axes of the slice: x: 4, y: 4, z: 8, core: 2. Of those that a mesh axis runs over, the one named last changes fastest.
Arguments:
- features: bfloat16 [32, 8, 1369, 1024], P('obj', 'view'), may hold values from -6 to 6
- projection: int32 [32, 8, 1369], P('obj'), may hold values from 0 to 1023, as said below
- active_count: int32 [32], P('obj'), may hold values from 512 to 1024, as said below
- in_weight: bfloat16 [1024, 768], replicated, may hold values from -0.1875 to 0.1875
- norm_gain: float32 [768], replicated, may hold values from 0.1 to 1.9
- qkv_weight: bfloat16 [768, 2304], replicated, may hold values from -4 to 4
- out_weight: bfloat16 [768, 768], replicated, may hold values from -0.21875 to 0.21875
- cotangent: bfloat16 [32, 1024, 768], P('obj', 'view'), may hold values from -6 to 6
Outputs:
- latent: bfloat16 [32, 1024, 768], P('obj', 'view')
- in_grad: float32 [1024, 768], P('view')
- qkv_grad: float32 [768, 2304], P('view')
- out_grad: float32 [768, 768], P('view')
Inputs may be any that keep to these rules, and one draw needn't show every extreme that they name: `projection`: every entry is below its object's active_count; in every object some live slots receive no patch. `active_count`: slots from this number on are empty: they are no keys, and their rows of latent are zero.
All inputs are finite; a program needn't handle non-finite values.
Results may differ from a plain program's by a relative error of at most 0.02.
Values may be sent and summed in bfloat16 or wider, within the bound.
A program may use at most 64 MiB of HBM per device.

v0:
```python
import jax
import jax.numpy as jnp
from jax import lax
from jax.sharding import PartitionSpec as P

HEAD_DIM = 64


def cut_along(value, dim, size):
    before, after = (value.shape[:dim], value.shape[dim + 1 :])
    return jnp.moveaxis(value.reshape(*before, size, -1, *after), dim, 0)


def sum_at_owner(value, axis, dim):
    size = lax.axis_size(axis)
    parts = lax.all_to_all(cut_along(value, dim, size), axis, 0, 0, tiled=True)
    return jnp.sum(parts, axis=0)


def side_by_side(arrays, axis, dim, along):
    ends, at = ([], 0)
    for a in arrays[:-1]:
        at += a.shape[along]
        ends.append(at)
    both = jnp.concatenate(arrays, axis=along)
    return tuple(jnp.split(lax.all_gather(both, axis, axis=dim, tiled=True), ends, axis=along))


def sent_and_summed(value, axis, dim):
    size = lax.axis_size(axis)
    parts = lax.all_to_all(cut_along(value, dim, size), axis, 0, 0, tiled=True)
    return jnp.sum(parts.astype(jnp.float32), axis=0)


def in_one_piece(arrays, axis, dim, along):
    widths = [a.shape[along] for a in arrays]
    both = jnp.concatenate(arrays, axis=along)
    result = lax.psum_scatter(both, axis, scatter_dimension=dim, tiled=True)
    return tuple(jnp.split(result, [sum(widths[:k]) for k in range(1, len(widths))], axis=along))


def packed_total(arrays, axis):
    flat, at, gathered = (jnp.concatenate([a.reshape(-1) for a in arrays]), 0, [])
    so_far = lax.psum(flat, axis)
    for a in arrays:
        gathered.append(so_far[at : at + a.size].reshape(a.shape))
        at += a.size
    return tuple(gathered)


def normalize(base_rows):
    center = jnp.mean(base_rows, axis=-1, keepdims=True)
    shifted = base_rows - center
    spread = jnp.mean(shifted * shifted, axis=-1, keepdims=True)
    inverse = lax.rsqrt(spread + 1e-06)
    return (shifted * inverse, inverse)


def per_device(
    features, projection, active_count, in_weight, norm_gain, qkv_weight, out_weight, cotangent
):
    groups = lax.axis_size("view")
    objects = lax.axis_size("obj")
    position = lax.axis_index("view")
    own_count = cotangent.shape[1]
    all_slots = own_count * groups
    width = out_weight.shape[0]
    heads = width // HEAD_DIM
    local_feat = features.reshape(features.shape[1] * features.shape[2], features.shape[3])
    local_rows = local_feat.shape[0]
    flat_proj = projection.reshape(projection.shape[1] * projection.shape[2])
    own_proj = lax.dynamic_slice_in_dim(flat_proj, position * local_rows, local_rows, 0)
    own_slots = position * own_count + lax.iota(jnp.int32, own_count)
    counts = jnp.sum((flat_proj[None, :] == own_slots[:, None]).astype(jnp.float32), axis=1)
    slot_ids = lax.iota(jnp.int32, own_count * lax.axis_size("view"))
    onehot = (own_proj[None, :] == slot_ids[:, None]).astype(jnp.bfloat16)
    totals = sum_at_owner(
        jnp.dot(onehot, local_feat, preferred_element_type=jnp.float32), "view", 0
    )
    voxels = (totals / jnp.maximum(counts, 1.0)[:, None]).astype(jnp.bfloat16)
    live_rows = (own_slots < active_count[0]).astype(jnp.float32)
    base_rows = jnp.dot(voxels, in_weight, preferred_element_type=jnp.float32)
    unit_rows, inverse = normalize(base_rows)
    normed = (unit_rows * norm_gain).astype(jnp.bfloat16)
    packed = jnp.dot(normed, qkv_weight, preferred_element_type=jnp.float32).astype(jnp.bfloat16)
    queries = packed[:, :width].reshape(own_count, heads, HEAD_DIM)
    key_all, value_all = side_by_side(
        (packed[:, width : 2 * width], packed[:, 2 * width :]), "view", 0, 1
    )
    key_heads = key_all.reshape(all_slots, heads, HEAD_DIM)
    value_heads = value_all.reshape(all_slots, heads, HEAD_DIM)
    inv_root = HEAD_DIM ** (-0.5)
    scores = (
        jnp.einsum("qhd,khd->hqk", queries, key_heads, preferred_element_type=jnp.float32)
        * inv_root
    )
    key_live = (lax.iota(jnp.int32, all_slots) < active_count[0])[None, None, :]
    masked = jnp.where(key_live, scores, -1e30)
    row_peak = jnp.max(masked, axis=-1, keepdims=True)
    expo_terms = jnp.where(key_live, jnp.exp(masked - row_peak), 0.0)
    weights = expo_terms / jnp.sum(expo_terms, axis=-1, keepdims=True)
    prob_rows = weights.astype(jnp.bfloat16)
    mixed_full = jnp.einsum(
        "hqk,khd->qhd", prob_rows, value_heads, preferred_element_type=jnp.float32
    )
    attended = mixed_full.reshape(own_count, width).astype(jnp.bfloat16)
    branch = jnp.dot(attended, out_weight, preferred_element_type=jnp.float32)
    latent = (live_rows[:, None] * (base_rows + branch)).astype(jnp.bfloat16)
    seed_rows = (cotangent[0].astype(jnp.float32) * live_rows[:, None] * (1.0 / objects)).astype(
        jnp.bfloat16
    )
    out_term = jnp.einsum("rc,rd->cd", attended, seed_rows, preferred_element_type=jnp.float32)
    grad_attended = jnp.einsum(
        "rd,cd->rc", seed_rows, out_weight, preferred_element_type=jnp.float32
    ).astype(jnp.bfloat16)
    grad_heads = grad_attended.reshape(own_count, heads, HEAD_DIM)
    grad_probs = jnp.einsum(
        "qhd,khd->hqk", grad_heads, value_heads, preferred_element_type=jnp.float32
    )
    delta_rows = jnp.sum(grad_heads.astype(jnp.float32) * mixed_full, axis=-1).T[:, :, None]
    grad_scores = (weights * (grad_probs - delta_rows) * inv_root).astype(jnp.bfloat16)
    grad_queries = jnp.einsum(
        "hqk,khd->qhd", grad_scores, key_heads, preferred_element_type=jnp.float32
    ).reshape(own_count, width)
    key_part = jnp.einsum(
        "hqk,qhd->khd", grad_scores, queries, preferred_element_type=jnp.float32
    ).reshape(own_count * lax.axis_size("view"), width)
    value_part = jnp.einsum(
        "hqk,qhd->khd", prob_rows, grad_heads, preferred_element_type=jnp.float32
    ).reshape(own_count * lax.axis_size("view"), width)
    key_grads = sent_and_summed(
        jnp.concatenate([key_part, value_part], axis=1).astype(jnp.bfloat16), "view", 0
    )
    grad_packed = jnp.concatenate([grad_queries, key_grads], axis=1).astype(jnp.bfloat16)
    qkv_term = jnp.einsum("rc,rd->cd", normed, grad_packed, preferred_element_type=jnp.float32)
    grad_normed = jnp.einsum(
        "rd,cd->rc", grad_packed, qkv_weight, preferred_element_type=jnp.float32
    )
    grad_unit = grad_normed * norm_gain
    grad_branch = inverse * (
        grad_unit
        - jnp.mean(grad_unit, axis=-1, keepdims=True)
        - unit_rows * jnp.mean(grad_unit * unit_rows, axis=-1, keepdims=True)
    )
    grad_base = (seed_rows.astype(jnp.float32) + grad_branch).astype(jnp.bfloat16)
    in_term = jnp.einsum("rc,rd->cd", voxels, grad_base, preferred_element_type=jnp.float32)
    in_share, qkv_share, out_share = (
        lax.psum_scatter(
            in_term.astype(jnp.bfloat16), "view", scatter_dimension=0, tiled=True
        ).astype(jnp.float32),
        *tuple(
            (
                part.astype(jnp.float32)
                for part in in_one_piece(
                    (qkv_term.astype(jnp.bfloat16), out_term.astype(jnp.bfloat16)), "view", 0, 1
                )
            )
        ),
    )
    in_grad, qkv_grad, out_grad = tuple(
        (
            part.astype(jnp.float32)
            for part in packed_total(
                (
                    in_share.astype(jnp.bfloat16),
                    qkv_share.astype(jnp.bfloat16),
                    out_share.astype(jnp.bfloat16),
                ),
                "obj",
            )
        )
    )
    return (latent[None], in_grad, qkv_grad, out_grad)


def solution(mesh):
    return jax.shard_map(
        per_device,
        mesh=mesh,
        in_specs=(
            P("obj", "view", None, None),
            P("obj", None, None),
            P("obj"),
            P(),
            P(),
            P(),
            P(),
            P("obj", "view", None),
        ),
        out_specs=(P("obj", "view", None), P("view", None), P("view", None), P("view", None)),
        check_vma=False,
    )
```

profile of v0, /device:TPU:1, one launch (start us, length us, event | category | flops | bytes accessed | tf_op | source)
XLA Modules:
  0.0 440.8 jit_solution(9661698597586454469)
XLA Ops:
  9.6 7.0 %fusion.1 = f32[8,128,1024]{2,1,0:T(8,128)} fusion(bf16[1,1,1369,1024]{3,2,1,0:T(8,128)(2,1)} %param.8, s32[8,128]{1,0:T(8,128)S(1)} %multiply_add_fusion, s32[1369]{0:T(1024)S(1)} %dynamic_slice.3), kind=kOutput, calls=%fused_computation.4 | convolution fusion | flops 2872402944 | bytes 7007588 | tf_op jit(solution)/shard_map/dot_general | solution.py:78
  16.6 7.6 %all-to-all-start = ((f32[8,128,1024]{2,1,0:T(8,128)}), f32[8,128,1024]{2,1,0:T(8,128)}, u32[]{:S(2)}, u32[]{:S(2)}) async-start(f32[8,128,1024]{2,1,0:T(8,128)} %fusion.1), calls=%async_computation | async-start | bytes 8388608 | tf_op jit(solution)/shard_map/all_to_all | solution.py:16
  24.2 5.2 %convert_reduce_fusion = f32[128]{0:T(128)S(1)} fusion(s32[128]{0:T(128)S(1)} %iota_add_fusion, s32[10952]{0:T(1024)} %reshape.146), kind=kLoop, calls=%fused_computation.6 | loop fusion | flops 4205440 | bytes 44832 | tf_op jit(solution)/shard_map/reduce_sum | solution.py:74
  29.5 43.6 %all-to-all-done = f32[8,128,1024]{2,1,0:T(8,128)} async-done(((f32[8,128,1024]{2,1,0:T(8,128)}), f32[8,128,1024]{2,1,0:T(8,128)}, u32[]{:S(2)}, u32[]{:S(2)}) %all-to-all-start) | async-done | bytes 4194336 | tf_op jit(solution)/shard_map/all_to_all | solution.py:16
  73.0 3.4 reduce_sum.81
  82.3 2.6 convolution_convert_fusion.6
  90.5 21.4 %all-gather.2.cloned.1.call-done = bf16[1024,1536]{1,0:T(8,128)(2,1)} async-done(((bf16[128,1536]{1,0:T(8,128)(2,1)}), bf16[1024,1536]{1,0:T(8,128)(2,1)}) %all-gather.2.cloned.1.call-update) | async-done | bytes 3145744 | tf_op jit(solution)/shard_map/all_gather | solution.py:26
  112.0 3.8 fusion.40
  115.7 2.6 copy.37
  118.3 2.6 copy.35
  120.9 6.6 %fusion.42 = (f32[12,128]{1,0:T(8,128)S(1)}, f32[12,128,1024]{2,1,0:T(8,128)}) fusion(pred[1024]{0:T(1024)(128)(4,1)} %iota_compare_fusion, bf16[128,12,64]{0,2,1:T(8,128)(2,1)} %bitcast.86, bf16[1024,12,64]{0,2,1:T(8,128)(2,1)} %bitcast.71), kind=kOutput, calls=%fused_computation.79 | convolution fusion | flops 209191936 | bytes 8068096 | tf_op jit(solution)/shard_map/sub | solution.py:100
  127.5 3.6 fusion.10
  140.5 4.6 %all-to-all-start.1 = ((bf16[8,128,1536]{1,2,0:T(8,128)(2,1)}), bf16[8,128,1536]{1,2,0:T(8,128)(2,1)}, u32[]{:S(2)}, u32[]{:S(2)}) async-start(bf16[8,128,1536]{1,2,0:T(8,128)(2,1)} %pad_maximum_fusion.1), calls=%async_computation.1 | async-start | bytes 6291456 | tf_op jit(solution)/shard_map/all_to_all | solution.py:31
  145.3 4.2 convolution_convert_fusion.7
  149.5 33.2 %all-to-all-done.1 = bf16[8,128,1536]{1,2,0:T(8,128)(2,1)} async-done(((bf16[8,128,1536]{1,2,0:T(8,128)(2,1)}), bf16[8,128,1536]{1,2,0:T(8,128)(2,1)}, u32[]{:S(2)}, u32[]{:S(2)}) %all-to-all-start.1) | async-done | bytes 3145760 | tf_op jit(solution)/shard_map/all_to_all | solution.py:31
  182.7 3.2 reduce
  185.9 2.7 fusion.39
  192.2 2.4 convolution_convert_fusion
  194.6 2.8 pad_maximum_fusion
  197.5 26.3 %reduce-scatter.3.cloned.1.call-done = bf16[128,768]{1,0:T(8,128)(2,1)} async-done(((bf16[1024,768]{1,0:T(8,128)(2,1)}), bf16[128,768]{1,0:T(8,128)(2,1)}) %reduce-scatter.3.cloned.1.call-update) | async-done | bytes 196624 | tf_op jit(solution)/shard_map/reduce_scatter | solution.py:148
  225.6 40.9 %reduce-scatter.5.cloned.1.call-done = bf16[96,3072]{1,0:T(8,128)(2,1)} async-done(((bf16[768,3072]{1,0:T(8,128)(2,1)}), bf16[96,3072]{1,0:T(8,128)(2,1)}) %reduce-scatter.5.cloned.1.call-update) | async-done | bytes 589840 | tf_op jit(solution)/shard_map/reduce_scatter | solution.py:38
  268.3 2.3 reshape.154
  276.0 2.4 fusion.13
  278.4 144.7 %all-reduce.2.cloned.1.call-done = bf16[393216]{0:T(1024)(128)(2,1)} async-done(((bf16[393216]{0:T(1024)(128)(2,1)}), bf16[393216]{0:T(1024)(128)(2,1)}) %all-reduce.2.cloned.1.call-update) | async-done | bytes 786448 | tf_op jit(solution)/shard_map/psum | solution.py:44
  (86 shorter events, 46.4 us)
Async XLA Ops:
  7.2 72.1 %copy-start = (bf16[768,2304]{1,0:T(8,128)(2,1)S(1)}, bf16[768,2304]{1,0:T(8,128)(2,1)}, u32[]{:S(2)}) copy-start(bf16[768,2304]{1,0:T(8,128)(2,1)} %param.13) | copy-start | bytes 10616836
  16.6 56.4 %all-to-all-start = ((f32[8,128,1024]{2,1,0:T(8,128)}), f32[8,128,1024]{2,1,0:T(8,128)}, u32[]{:S(2)}, u32[]{:S(2)}) async-start(f32[8,128,1024]{2,1,0:T(8,128)} %fusion.1), calls=%async_computation | async-start | bytes 8388608 | tf_op jit(solution)/shard_map/all_to_all | solution.py:16
  24.2 87.7 %all-gather.2.cloned.1.call-start = ((), (), s32[]{:S(2)}) async-start(), calls=%async_computation.4 | async-start | bytes 3538944 | tf_op jit(solution)/shard_map/all_gather | solution.py:26
  29.5 49.1 %copy-start.15 = (f32[128]{0:T(128)}, f32[128]{0:T(128)S(1)}, u32[]{:S(2)}) copy-start(f32[128]{0:T(128)S(1)} %broadcast_maximum_fusion) | copy-start | bytes 1540
  29.5 49.8 %copy-start.10 = (f32[768]{0:T(1024)S(1)}, f32[768]{0:T(1024)}, u32[]{:S(2)}) copy-start(f32[768]{0:T(1024)} %param.12) | copy-start | bytes 9220
  79.3 3.0 copy-start.13
  80.0 0.8 copy-start.5
  82.3 33.5 %copy-start.11 = (f32[128]{0:T(128)}, f32[128]{0:T(128)S(1)}, u32[]{:S(2)}) copy-start(f32[128]{0:T(128)S(1)} %compare_convert_fusion) | copy-start | bytes 1540
  127.4 3.6 copy-start.6
  131.0 1.4 copy-start.4
  131.0 3.9 slice-start
  132.4 2.6 slice-start.1
  135.0 1.7 copy-start.7
  136.8 1.7 copy-start.1
  140.5 42.2 %all-to-all-start.1 = ((bf16[8,128,1536]{1,2,0:T(8,128)(2,1)}), bf16[8,128,1536]{1,2,0:T(8,128)(2,1)}, u32[]{:S(2)}, u32[]{:S(2)}) async-start(bf16[8,128,1536]{1,2,0:T(8,128)(2,1)} %pad_maximum_fusion.1), calls=%async_computation.1 | async-start | bytes 6291456 | tf_op jit(solution)/shard_map/all_to_all | solution.py:31
  145.1 40.8 %copy-start.14 = (f32[128]{0:T(128)S(1)}, f32[128]{0:T(128)}, u32[]{:S(2)}) copy-start(f32[128]{0:T(128)} %copy-done.13) | copy-start | bytes 1540
  145.1 78.6 %reduce-scatter.3.cloned.1.call-start = ((), (), s32[]{:S(2)}) async-start(), calls=%async_computation.5 | async-start | bytes 1769472 | tf_op jit(solution)/shard_map/reduce_scatter | solution.py:148
  185.9 2.7 copy-start.3
  185.9 2.7 copy-start.8
  185.9 2.7 copy-start.9
  185.9 2.8 copy-start.12
  185.9 2.8 copy-start.16
  190.6 75.8 %reduce-scatter.5.cloned.1.call-start = ((), (), s32[]{:S(2)}) async-start(), calls=%async_computation.6 | async-start | bytes 5308416 | tf_op jit(solution)/shard_map/reduce_scatter | solution.py:38
  197.4 225.8 %all-reduce.2.cloned.1.call-start = ((), (), s32[]{:S(2)}) async-start(), calls=%async_computation.7 | async-start | bytes 1572864 | tf_op jit(solution)/shard_map/psum | solution.py:44
  (1 other events, 0.7 us)
Sparse Core Ops, SparseCore 0:
  81.7 30.1 all-gather.1
  190.7 32.9 reduce-scatter.2
  226.3 40.0 reduce-scatter.4
  276.1 147.0 all-reduce.1
where the time goes:
time: 446 us; the launch traced here: 441 us
  waiting for transfers between devices  310 us (70%)
  matrix products  38.9 us (9%)
  local copies, waits for them, and re-layouts  36.4 us (8%)
  other arithmetic  28.1 us (6%)
  between operations  14.7 us (3%)
  starting transfers between devices  12.4 us (3%)
    psum x1, waiting for transfers between devices, packed_total(): so_far = lax.psum(flat, axis)  145 us
    all_to_all x1, waiting for transfers between devices, sum_at_owner(): parts = lax.all_to_all(cut_along(value, dim, size), axis, 0, 0, tiled=True)  43.6 us
    reduce_scatter x1, waiting for transfers between devices, in_one_piece(): result = lax.psum_scatter(both, axis, scatter_dimension=dim, tiled=True)  40.9 us
    all_to_all x1, waiting for transfers between devices, sent_and_summed(): parts = lax.all_to_all(cut_along(value, dim, size), axis, 0, 0, tiled=True)  33.2 us
    reduce_scatter x1, waiting for transfers between devices, per_device(): lax.psum_scatter(in_term.astype(jnp.bfloat16), 'view', scatter_dimension=...  26.3 us
    all_gather x1, waiting for transfers between devices, side_by_side(): lax.all_gather(both, axis, axis=dim, tiled=True)  21.4 us
  transfers between devices with their start and end apart: 6, of which 6 were waited for; matrix products, arithmetic and copies ran while one was open for 6% of the time, Pallas kernels for 0%

commit v1 on v0

v1 whole, which is shorter than its diff:
```python
import jax
import jax.numpy as jnp
from jax import lax
from jax.experimental import pallas as pl
from jax.experimental.pallas import tpu as pltpu
from jax.sharding import PartitionSpec as P

HEAD_DIM = 64
MESH = pl.DeviceIdType.MESH
F32 = jnp.float32
BF16 = jnp.bfloat16
NEG = -1e30
CHUNKS = 4
QROWS = 256


def dot_nn(a, b):
    return lax.dot_general(a, b, (((1,), (0,)), ((), ())), preferred_element_type=F32)


def dot_nt(a, b):
    return lax.dot_general(a, b, (((1,), (1,)), ((), ())), preferred_element_type=F32)


def dot_tn(a, b):
    return lax.dot_general(a, b, (((0,), (0,)), ((), ())), preferred_element_type=F32)


def make_kernel(sizes):
    patches, feat, width, own, objects, views = sizes
    chips = 4
    heads = 3
    part = heads * HEAD_DIM
    group = chips * own
    slots = 2 * group
    cols = feat // CHUNKS
    vcols = feat // chips
    orows = part // 2

    def kernel(
        feat_hbm, proj_ref, count_ref, in_hbm, gain_ref, qkv_hbm, out_hbm, cot_hbm,
        latent_ref, gin_ref, gmain_ref,
        feat_v, inw, qkvw, outw, cot_v, hot, psend, precv, pown, ysend, yrecv,
        seeds, vox, vcol, base, unit, normed, wown, qs, kvs, gouts, att, attr, afull,
        dkv, dkv_send, dkv_recv, gp, gpr, gpfull, og, og_send, og_recv,
        qg, qg_send, qg_recv, qsum, qrecv, gball, ig, ig_send, ig_recv,
        mx, mxr, mz, mzr, mf, mg, ix, ixr, iz, izr, jf, jg,
        ssem, rsem, lsem,
    ):
        obj = lax.axis_index("obj")
        view = lax.axis_index("view")
        c = view // 2
        k = view % 2
        z = obj // 4
        x = obj % 4

        def at_y(d):
            return (obj, ((c + d) % 4) * 2 + k)

        def at_x(d):
            return (z * 4 + (x + d) % 4, view)

        def at_z(d):
            return (((z + d) % 8) * 4 + x, view)

        mate = (obj, c * 2 + (1 - k))
        used = [0]
        sent = []

        def send(src, dst, device):
            n = used[0]
            used[0] += 1
            cp = pltpu.make_async_remote_copy(
                src_ref=src, dst_ref=dst, send_sem=ssem.at[n], recv_sem=rsem.at[n],
                device_id=device, device_id_type=MESH,
            )
            cp.start()
            sent.append(cp)
            return cp

        def load(n, src, dst):
            cp = pltpu.make_async_copy(src, dst, lsem.at[n])
            cp.start()
            return cp

        barrier = pltpu.get_barrier_semaphore()
        peers = [mate]
        peers += [at_y(d) for d in (1, 2, 3)]
        peers += [at_x(d) for d in (1, 2, 3)]
        peers += [at_z(d) for d in range(1, 8)]
        for p in peers:
            pl.semaphore_signal(barrier, 1, device_id=p, device_id_type=MESH)

        l_cot = load(0, cot_hbm, cot_v)
        l_feat = load(1, feat_hbm, feat_v)
        l_out = load(2, out_hbm, outw)
        l_in = load(3, in_hbm, inw)
        l_qkv = load(4, qkv_hbm, qkvw)

        count = count_ref[0]
        own_ids = view * own + lax.broadcasted_iota(jnp.int32, (own, 1), 0)
        live = jnp.where(own_ids < count, 1.0, 0.0).astype(F32)
        proj_row = proj_ref[pl.ds(view, 1), :]
        for kk in range(2):
            par = k if kk else 1 - k
            for d in range(4):
                ids = (
                    ((c + 4 - d) % 4) * (2 * own)
                    + par * own
                    + lax.broadcasted_iota(jnp.int32, (own, patches), 0)
                )
                hot[kk, own * d : own * (d + 1), :] = jnp.where(ids == proj_row, 1.0, 0.0).astype(BF16)

        l_cot.wait()
        seeds[0:own, :] = (cot_v[...].astype(F32) * live * (1.0 / objects)).astype(BF16)
        pl.semaphore_wait(barrier, len(peers))
        seed_cp = [
            send(seeds.at[pl.ds(0, own)], seeds.at[pl.ds(own * d, own)], at_y(d)) for d in (1, 2, 3)
        ]

        l_feat.wait()
        mate_cp, y_cp = [], []

        def pass_on(j):
            mate_cp[j].wait_recv()
            both = pown[j] + precv[j].astype(F32)
            pown[j] = both
            ysend[j] = both.astype(BF16)
            y_cp.append(
                [
                    send(ysend.at[j, pl.ds(own * d, own)], yrecv.at[d - 1, j], at_y(4 - d))
                    for d in (1, 2, 3)
                ]
            )

        for j in range(CHUNKS):
            block = feat_v[:, cols * j : cols * (j + 1)]
            psend[j] = dot_nn(hot[0], block).astype(BF16)
            mate_cp.append(send(psend.at[j], precv.at[j], mate))
            pown[j] = dot_nn(hot[1], block)
            if j > 0:
                pass_on(j - 1)
        pass_on(CHUNKS - 1)

        number = jnp.zeros((own, 1), F32)
        for w in range(views):
            same = proj_ref[w : w + 1, :] == view * own + lax.broadcasted_iota(
                jnp.int32, (own, patches), 0
            )
            number += jnp.sum(jnp.where(same, 1.0, 0.0), axis=1, keepdims=True)
        number = jnp.maximum(number, 1.0)

        l_qkv.wait()
        for t in range(3):
            window = qkvw[:, pl.ds(pl.multiple_of(width * t + 128 * ((3 * c) // 2), 128), 256)]

            @pl.when(c % 2 == 0)
            def _():
                wown[:, part * t : part * (t + 1)] = window[:, 0:part]

            @pl.when(c % 2 == 1)
            def _():
                wown[:, part * t : part * (t + 1)] = window[:, 64 : 64 + part]

        l_out.wait()
        rows = outw[pl.ds(pl.multiple_of(part * c, 64), part), :]
        gouts[0:own, :] = dot_nt(seeds[0:own, :], rows).astype(BF16)
        for d in (1, 3, 2):
            seed_cp[d - 1].wait_recv()
            gouts[own * d : own * (d + 1), :] = dot_nt(seeds[own * d : own * (d + 1), :], rows).astype(BF16)

        for j in range(CHUNKS):
            total = pown[j, 0:own, :]
            for d in (1, 3, 2):
                y_cp[j][d - 1].wait_recv()
                total += yrecv[d - 1, j].astype(F32)
            vox[:, cols * j : cols * (j + 1)] = (total / number).astype(BF16)
        l_in.wait()
        base_rows = dot_nn(vox[...], inw[...])
        base[...] = base_rows
        shifted = base_rows - jnp.mean(base_rows, axis=1, keepdims=True)
        spread = jnp.mean(shifted * shifted, axis=1, keepdims=True)
        inverse = lax.rsqrt(spread + 1e-06)
        unit_rows = shifted * inverse
        unit[...] = unit_rows
        gain = gain_ref[...]
        normed[0:own, :] = (unit_rows * gain).astype(BF16)
        n_cp = [
            send(normed.at[pl.ds(0, own)], normed.at[pl.ds(own * d, own)], at_y(d)) for d in (1, 2, 3)
        ]
        v_cp = [
            send(
                vox.at[:, pl.ds(pl.multiple_of(vcols * ((c + d) % 4), 128), vcols)],
                vcol.at[pl.ds(own * d, own)],
                at_y(d),
            )
            for d in (1, 2, 3)
        ]
        vcol[0:own, :] = vox[:, pl.ds(pl.multiple_of(vcols * c, 128), vcols)]

        kv_cp = []
        for d in (0, 1, 3, 2):
            if d:
                n_cp[d - 1].wait_recv()
            at = slice(own * d, own * (d + 1))
            packed = dot_nn(normed[at, :], wown[...])
            qs[at, :] = (packed[:, 0:part] * (HEAD_DIM**-0.5)).astype(BF16)
            kvs[at, :] = packed[:, part : 3 * part].astype(BF16)
            kv_cp.append(
                send(kvs.at[pl.ds(own * d, own)], kvs.at[pl.ds(group + own * d, own)], mate)
            )

        lane = lax.broadcasted_iota(jnp.int32, (1, own), 1)
        pieces = []
        for par in (k, 1 - k):
            for d in range(4):
                ids = ((c + 4 - d) % 4) * (2 * own) + par * own + lane
                pieces.append(jnp.where(ids < count, 0.0, NEG).astype(F32))
        bias = jnp.concatenate(pieces, axis=1)
        for cp in kv_cp:
            cp.wait_recv()

        dkv_cp = []
        for h in range(heads):
            hs = slice(HEAD_DIM * h, HEAD_DIM * (h + 1))
            keys = kvs[:, hs]
            values = kvs[:, part + HEAD_DIM * h : part + HEAD_DIM * (h + 1)]
            grad_k = jnp.zeros((slots, HEAD_DIM), F32)
            grad_v = jnp.zeros((slots, HEAD_DIM), F32)
            for b in range(group // QROWS):
                rs = slice(QROWS * b, QROWS * (b + 1))
                q = qs[rs, hs]
                go = gouts[rs, hs]
                s = dot_nt(q, keys) + bias
                e = jnp.exp(s - jnp.max(s, axis=1, keepdims=True))
                w = e * (1.0 / jnp.sum(e, axis=1, keepdims=True))
                p = w.astype(BF16)
                mixed = dot_nn(p, values)
                att[rs, hs] = mixed.astype(BF16)
                delta = jnp.sum(go.astype(F32) * mixed, axis=1, keepdims=True)
                gs = (w * (dot_nt(go, values) - delta)).astype(BF16)
                gp[rs, hs] = (dot_nn(gs, keys) * (HEAD_DIM**-0.5)).astype(BF16)
                grad_k += dot_tn(gs, q)
                grad_v += dot_tn(p, go)
            both = jnp.concatenate([grad_k, grad_v], axis=1)
            dkv[h] = both[0:group]
            dkv_send[h] = both[group:].astype(BF16)
            dkv_cp.append(send(dkv_send.at[h], dkv_recv.at[h], mate))

        a_cp = [
            send(att.at[pl.ds(own * d, own)], attr.at[c], at_y(4 - d)) for d in (1, 2, 3)
        ]
        attr[c] = att[0:own, :]
        og[...] = dot_tn(att[...], seeds[...])
        og_send[...] = og[pl.ds(pl.multiple_of(orows * (1 - k), 32), orows), :].astype(BF16)
        og_cp = send(og_send, og_recv, mate)

        for h in range(heads):
            dkv_cp[h].wait_recv()
            both = dkv[h] + dkv_recv[h].astype(F32)
            gp[:, part + HEAD_DIM * h : part + HEAD_DIM * (h + 1)] = both[:, 0:HEAD_DIM].astype(BF16)
            gp[:, 2 * part + HEAD_DIM * h : 2 * part + HEAD_DIM * (h + 1)] = both[:, HEAD_DIM:].astype(BF16)
        g_cp = [send(gp.at[pl.ds(own * d, own)], gpr.at[c], at_y(4 - d)) for d in (1, 2, 3)]
        gpr[c] = gp[0:own, :]

        whole = dot_tn(normed[...], gp[...])
        for t in range(8):
            qg[t] = whole[orows * t : orows * (t + 1), :]
        for t in range(4):
            qg_send[t] = qg[2 * t + (1 - k)].astype(BF16)
        qg_cp = send(qg_send, qg_recv, mate)

        for t in range(4):
            a_at = slice(part * t, part * (t + 1))
            if t == 0:
                for cp in a_cp:
                    cp.wait_recv()
            afull[:, a_at] = attr[t]
        branch = dot_nn(afull[...], outw[...])
        latent_ref[...] = (live * (base[...] + branch)).astype(BF16)

        og_cp.wait_recv()
        og_sum = (
            og[pl.ds(pl.multiple_of(orows * k, 32), orows), :] + og_recv[...].astype(F32)
        ).astype(BF16)
        for r in range(4):
            mx[3, r] = og_sum[24 * r : 24 * (r + 1), :]

        qg_cp.wait_recv()
        for t in range(4):
            qsum[t] = (qg[2 * t + k] + qg_recv[t].astype(F32)).astype(BF16)
        t_cp = [send(qsum.at[(c + d) % 4], qrecv.at[c], at_y(d)) for d in (1, 2, 3)]
        qrecv[c] = qsum[c]

        for cp in g_cp:
            cp.wait_recv()
        for t in range(4):
            for s3 in range(3):
                gpfull[:, width * s3 + part * t : width * s3 + part * (t + 1)] = gpr[
                    t, :, part * s3 : part * (s3 + 1)
                ]
        grad_unit = dot_nt(gpfull[...], qkvw[...]) * gain
        unit_rows = unit[...]
        branch_grad = inverse * (
            grad_unit
            - jnp.mean(grad_unit, axis=1, keepdims=True)
            - unit_rows * jnp.mean(grad_unit * unit_rows, axis=1, keepdims=True)
        )
        gball[0:own, :] = (seeds[0:own, :].astype(F32) + branch_grad).astype(BF16)
        b_cp = [
            send(gball.at[pl.ds(0, own)], gball.at[pl.ds(own * d, own)], at_y(d)) for d in (1, 2, 3)
        ]

        for cp in t_cp:
            cp.wait_recv()
        for t in range(4):
            for s3 in range(3):
                for r in range(4):
                    mx[s3, r, :, part * t : part * (t + 1)] = qrecv[
                        t, 24 * r : 24 * (r + 1), part * s3 : part * (s3 + 1)
                    ]

        def x_scatter(buf, recv):
            return [send(buf.at[(x + d) % 4], recv.at[d - 1], at_x(d)) for d in (1, 2, 3)]

        def x_sum(buf, recv, cps, out):
            for cp in cps:
                cp.wait_recv()
            out[...] = (
                buf[x].astype(F32)
                + recv[0].astype(F32)
                + recv[1].astype(F32)
                + recv[2].astype(F32)
            ).astype(BF16)

        half = width // 2

        def z_piece(buf, where):
            return buf.at[where // 2, :, pl.ds(pl.multiple_of(half * (where % 2), 128), half)]

        def z_scatter(buf, recv):
            return [send(z_piece(buf, (z + d) % 8), recv.at[d - 1], at_z(d)) for d in range(1, 8)]

        def z_sum(buf, recv, cps, out):
            total = z_piece(buf, z)[...].astype(F32)
            for d in range(1, 8):
                cps[d - 1].wait_recv()
                total += recv[d - 1].astype(F32)
            out[...] = total.astype(BF16)

        def z_gather(fin, full):
            cps = [send(fin, z_piece(full.at[x], z), at_z(d)) for d in range(1, 8)]
            full[x, z // 2, :, pl.ds(pl.multiple_of(half * (z % 2), 128), half)] = fin[...]
            return cps

        def x_gather(full, cps):
            for cp in cps:
                cp.wait_recv()
            return [send(full.at[x], full.at[x], at_x(d)) for d in (1, 2, 3)]

        mx_cp = x_scatter(mx, mxr)

        for cp in v_cp + b_cp:
            cp.wait_recv()
        ig[...] = dot_tn(vcol[...], gball[...])
        ig_send[...] = ig[pl.ds(pl.multiple_of(own * (1 - k), 128), own), :].astype(BF16)
        ig_cp = send(ig_send, ig_recv, mate)
        ig_cp.wait_recv()
        ig_sum = (
            ig[pl.ds(pl.multiple_of(own * k, 128), own), :] + ig_recv[...].astype(F32)
        ).astype(BF16)
        for t in range(4):
            for r in range(4):
                ix[t, r] = ig_sum[32 * t + 8 * r : 32 * t + 8 * (r + 1), :]
        ix_cp = x_scatter(ix, ixr)

        x_sum(mx, mxr, mx_cp, mz)
        mz_cp = z_scatter(mz, mzr)
        x_sum(ix, ixr, ix_cp, iz)
        iz_cp = z_scatter(iz, izr)
        z_sum(mz, mzr, mz_cp, mf)
        mg_cp = z_gather(mf, mg)
        z_sum(iz, izr, iz_cp, jf)
        jg_cp = z_gather(jf, jg)
        mo_cp = x_gather(mg, mg_cp)
        jo_cp = x_gather(jg, jg_cp)
        for cp in mo_cp:
            cp.wait_recv()
        gmain_ref[...] = mg[...]
        for cp in jo_cp:
            cp.wait_recv()
        gin_ref[...] = jg[...]
        for cp in sent:
            cp.wait_send()

    scratch = [
        ((patches, feat), BF16), ((feat, width), BF16), ((width, 3 * width), BF16),
        ((width, width), BF16), ((own, width), BF16), ((2, group, patches), BF16),
        ((CHUNKS, group, cols), BF16), ((CHUNKS, group, cols), BF16), ((CHUNKS, group, cols), F32),
        ((CHUNKS, group, cols), BF16), ((3, CHUNKS, own, cols), BF16),
        ((group, width), BF16), ((own, feat), BF16), ((group, vcols), BF16),
        ((own, width), F32), ((own, width), F32), ((group, width), BF16),
        ((width, 3 * part), BF16), ((group, part), BF16), ((slots, 2 * part), BF16),
        ((group, part), BF16), ((group, part), BF16), ((4, own, part), BF16), ((own, width), BF16),
        ((heads, group, 128), F32), ((heads, group, 128), BF16), ((heads, group, 128), BF16),
        ((group, 3 * part), BF16), ((4, own, 3 * part), BF16), ((own, 3 * width), BF16),
        ((part, width), F32), ((orows, width), BF16), ((orows, width), BF16),
        ((8, orows, 3 * part), F32), ((4, orows, 3 * part), BF16), ((4, orows, 3 * part), BF16),
        ((4, orows, 3 * part), BF16), ((4, orows, 3 * part), BF16),
        ((group, width), BF16), ((2 * own, width), F32), ((own, width), BF16), ((own, width), BF16),
        ((4, 4, 24, width), BF16), ((3, 4, 24, width), BF16), ((4, 24, width), BF16),
        ((7, 24, width // 2), BF16), ((24, width // 2), BF16), ((4, 4, 24, width), BF16),
        ((4, 4, 8, width), BF16), ((3, 4, 8, width), BF16), ((4, 8, width), BF16),
        ((7, 8, width // 2), BF16), ((8, width // 2), BF16), ((4, 4, 8, width), BF16),
    ]
    return kernel, scratch


def per_device(
    features, projection, active_count, in_weight, norm_gain, qkv_weight, out_weight, cotangent
):
    patches, feat = features.shape[2:]
    own, width = cotangent.shape[1:]
    views = projection.shape[1]
    objects = lax.axis_size("obj")
    kernel, scratch = make_kernel((patches, feat, width, own, objects, views))
    vmem = pl.BlockSpec(memory_space=pltpu.VMEM)
    hbm = pl.BlockSpec(memory_space=pl.ANY)
    latent, gin, gmain = pl.pallas_call(
        kernel,
        name="encode",
        out_shape=(
            jax.ShapeDtypeStruct((own, width), BF16),
            jax.ShapeDtypeStruct((4, 4, 8, width), BF16),
            jax.ShapeDtypeStruct((4, 4, 24, width), BF16),
        ),
        in_specs=[hbm, vmem, pl.BlockSpec(memory_space=pltpu.SMEM), hbm, vmem, hbm, hbm, hbm],
        out_specs=(vmem, vmem, vmem),
        scratch_shapes=[pltpu.VMEM(s, t) for s, t in scratch]
        + [
            pltpu.SemaphoreType.DMA((96,)),
            pltpu.SemaphoreType.DMA((96,)),
            pltpu.SemaphoreType.DMA((5,)),
        ],
        compiler_params=pltpu.CompilerParams(
            collective_id=0, has_side_effects=True, vmem_limit_bytes=62 * 1024 * 1024
        ),
    )(
        features.reshape(patches, feat),
        projection.reshape(views, patches),
        active_count,
        in_weight,
        norm_gain.reshape(1, width),
        qkv_weight,
        out_weight,
        cotangent.reshape(own, width),
    )
    gmain = gmain.reshape(4, 96, width)
    qkv_grad = jnp.concatenate([gmain[0], gmain[1], gmain[2]], axis=1).astype(F32)
    return (
        latent[None],
        gin.reshape(own, width).astype(F32),
        qkv_grad,
        gmain[3].astype(F32),
    )


def solution(mesh):
    return jax.shard_map(
        per_device,
        mesh=mesh,
        in_specs=(
            P("obj", "view", None, None),
            P("obj", None, None),
            P("obj"),
            P(),
            P(),
            P(),
            P(),
            P("obj", "view", None),
        ),
        out_specs=(P("obj", "view", None), P("view", None), P("view", None), P("view", None)),
        check_vma=False,
    )
```

time: 446 us -> 116 us (0.26); the launches traced: 441 us -> 115 us
  waiting for transfers between devices: 310 us -> 0 us
  Pallas kernels: 0 us -> 108 us
  matrix products: 38.9 us -> 0 us
  local copies, waits for them, and re-layouts: 36.4 us -> 3.17 us
  other arithmetic: 28.1 us -> 2.5 us
  between operations: 14.7 us -> 1.31 us
  starting transfers between devices: 12.4 us -> 0 us
    psum x1 -> x0, waiting for transfers between devices: 145 us -> none  [packed_total(): so_far = lax.psum(flat, axis)]
    pallas_call x0 -> x1, Pallas kernels: none -> 108 us  [per_device(): pl.pallas_call(kernel, name='encode', out_shape=(jax.ShapeDtypeStruct((ow...]
    all_to_all x2 -> x0, waiting for transfers between devices: 76.8 us -> none  [the longest x1 43.6 us: sum_at_owner(): parts = lax.all_to_all(cut_along(value, dim, size), axis, 0, 0, tiled=True)]
    reduce_scatter x2 -> x0, waiting for transfers between devices: 67.2 us -> none  [the longest x1 40.9 us: in_one_piece(): result = lax.psum_scatter(both, axis, scatter_dimension=dim, tiled=True)]
    dot_general x14 -> x0, matrix products: 32.3 us -> none  [the longest x1 6.97 us: per_device(): jnp.dot(onehot, local_feat, preferred_element_type=jnp.float32)]
    all_gather x1 -> x0, waiting for transfers between devices: 21.4 us -> none  [side_by_side(): lax.all_gather(both, axis, axis=dim, tiled=True)]
    split x5 -> x0, local copies, waits for them, and re-layouts: 12.3 us -> none  [the longest x3 8.92 us: side_by_side(): jnp.split(lax.all_gather(both, axis, axis=dim, tiled=True), ends, axis=al...]
    all_to_all x2 -> x0, starting transfers between devices: 12.2 us -> none  [the longest x1 7.63 us: sum_at_owner(): parts = lax.all_to_all(cut_along(value, dim, size), axis, 0, 0, tiled=True)]
  transfers between devices with their start and end apart: 6 -> 0, of which waited for: 6 -> 0; matrix products, arithmetic and copies ran while one was open for 6% -> 0% of each run, Pallas kernels for 0% -> 0%
where the time goes in v1:
time: 116 us; the launch traced here: 115 us
  Pallas kernels  108 us (93%)
  local copies, waits for them, and re-layouts  3.17 us (3%)
  other arithmetic  2.5 us (2%)
  between operations  1.31 us (1%)
    pallas_call x1, Pallas kernels, per_device(): pl.pallas_call(kernel, name='encode', out_shape=(jax.ShapeDtypeStruct((ow...  108 us

profile of v1, /device:TPU:1, one launch (start us, length us, event | category | flops | bytes accessed | tf_op | source)
XLA Modules:
  0.0 115.4 jit_solution(12836081614625818434)
XLA Ops:
  0.6 1.3 %reshape.36.gain_ref = f32[1,768]{1,0:T(1,128)} reshape(f32[768]{0:T(1024)} %param.12) | data formatting | bytes 6144 | tf_op jit(solution)/shard_map/reshape | solution.py:453
  2.5 108.5 %encode.1 = (bf16[128,768]{1,0:T(8,128)(2,1)}, bf16[4,4,8,768]{3,2,1,0:T(8,128)(2,1)}, bf16[4,4,24,768]{3,2,1,0:T(8,128)(2,1)}) custom-call(bf16[1369,1024]{1,0:T(8,128)(2,1)} %bitcast.13, s32[8,1369]{1,0:T(8,128)} %bitcast.19, s32[1]{0:T(128)S(6)} %copy.13.count_ref, bf16[1024,768]{1,0:T(8,128)(2,1)} %in_hbm.1, f32[1,768]{1,0:T(1,128)} %reshape.36.gain_ref, ...), custom_call_target="tpu_custom_call" | custom-call | tf_op jit(solution)/shard_map/encode/pallas_call | solution.py:429
  111.0 0.0 copy-start.1
  111.0 0.0 copy-start
  111.0 1.2 %fusion = (bf16[1,4,24,768]{3,2,1,0:T(8,128)(2,1)S(1)}, bf16[1,4,24,768]{3,2,1,0:T(8,128)(2,1)S(1)}, bf16[1,4,24,768]{3,2,1,0:T(8,128)(2,1)S(1)}, bf16[1,4,24,768]{3,2,1,0:T(8,128)(2,1)S(1)}) fusion(bf16[4,4,24,768]{3,2,1,0:T(8,128)(2,1)} %get-tuple-element.9), kind=kLoop, calls=%fused_computation.3 | loop fusion | bytes 1179648 | tf_op jit(solution)/shard_map/slice | solution.py:464
  112.2 1.0 maximum_convert_fusion
  113.2 0.7 bitcast_convert_fusion.1
  114.0 0.0 copy-done.1
  114.0 0.8 bitcast_convert_fusion
  114.7 0.0 copy-done
  114.8 0.7 copy.14
Async XLA Ops:
  111.0 3.0 %copy-start.1 = (bf16[4,4,8,768]{3,2,1,0:T(8,128)(2,1)S(1)}, bf16[4,4,8,768]{3,2,1,0:T(8,128)(2,1)}, u32[]{:S(2)}) copy-start(bf16[4,4,8,768]{3,2,1,0:T(8,128)(2,1)} %get-tuple-element.8) | copy-start | bytes 589828
  111.0 3.7 %copy-start = (bf16[128,768]{1,0:T(8,128)(2,1)S(1)}, bf16[128,768]{1,0:T(8,128)(2,1)}, u32[]{:S(2)}) copy-start(bf16[128,768]{1,0:T(8,128)(2,1)} %get-tuple-element.7) | copy-start | bytes 589828

commit v2 on v1

v2 whole, which is shorter than its diff:
```python
import jax
import jax.numpy as jnp
from jax import lax
from jax.experimental import pallas as pl
from jax.experimental.pallas import tpu as pltpu
from jax.sharding import PartitionSpec as P

HEAD_DIM = 64
MESH = pl.DeviceIdType.MESH
F32 = jnp.float32
BF16 = jnp.bfloat16
NEG = -1e30
CHUNKS = 4
QROWS = 256


def dot_nn(a, b):
    return lax.dot_general(a, b, (((1,), (0,)), ((), ())), preferred_element_type=F32)


def dot_nt(a, b):
    return lax.dot_general(a, b, (((1,), (1,)), ((), ())), preferred_element_type=F32)


def dot_tn(a, b):
    return lax.dot_general(a, b, (((0,), (0,)), ((), ())), preferred_element_type=F32)


def make_kernel(sizes):
    patches, feat, width, own, objects, views = sizes
    chips = 4
    heads = 3
    part = heads * HEAD_DIM
    group = chips * own
    slots = 2 * group
    cols = feat // CHUNKS
    vcols = feat // chips
    orows = part // 2

    def kernel(
        feat_hbm, proj_ref, count_ref, in_hbm, gain_ref, qkv_hbm, out_hbm, cot_hbm,
        latent_ref, gin_ref, gmain_ref,
        feat_v, inw, qkvw, outw, cot_v, hot, psend, precv, pown, ysend, rrecv, yrecv,
        seeds, vox, vcol, base, unit, normed, turned, wown, qs, kvs, gsend, gouts, att, attr, afull,
        dkv, dkv_send, dkv_recv, gp, gpr, gpfull, og, og_send, og_recv,
        qg, qg_send, qg_recv, qsum, qrecv, joined, gball, ig, ig_send, ig_recv,
        mx, mxr, mz, mzr, mf, mg, ix, ixr, iz, izr, jf, jg,
        ssem, rsem, lsem,
    ):
        obj = lax.axis_index("obj")
        view = lax.axis_index("view")
        c = view // 2
        k = view % 2
        z = obj // 4
        x = obj % 4

        def at_y(d):
            return (obj, ((c + d) % 4) * 2 + k)

        def at_x(d):
            return (z * 4 + (x + d) % 4, view)

        def at_z(d):
            return (((z + d) % 8) * 4 + x, view)

        mate = (obj, c * 2 + (1 - k))
        used = [0]
        sent = []

        def send(src, dst, device):
            n = used[0]
            used[0] += 1
            cp = pltpu.make_async_remote_copy(
                src_ref=src, dst_ref=dst, send_sem=ssem.at[n], recv_sem=rsem.at[n],
                device_id=device, device_id_type=MESH,
            )
            cp.start()
            sent.append(cp)
            return cp

        def load(n, src, dst):
            cp = pltpu.make_async_copy(src, dst, lsem.at[n])
            cp.start()
            return cp

        def rows_of(d, half=None):
            if half is None:
                return pl.ds(own * d, own)
            return pl.ds(own * d + own // 2 * half, own // 2)

        def gather_start(buf):
            out = {}
            for to, slot, order in ((1, 1, (0, 1)), (3, 3, (1, 0))):
                for half in order:
                    out[slot, half] = send(
                        buf.at[rows_of(0, half)], buf.at[rows_of(slot, half)], at_y(to)
                    )
            return out

        def gather_pass(buf, cps):
            cps[1, 0].wait_recv()
            cps[2, 0] = send(buf.at[rows_of(1, 0)], buf.at[rows_of(2, 0)], at_y(1))
            cps[3, 1].wait_recv()
            cps[2, 1] = send(buf.at[rows_of(3, 1)], buf.at[rows_of(2, 1)], at_y(3))

        def gather_wait(cps, slot):
            for half in ((1,), (0, 1), (0,))[slot - 1]:
                cps[slot, half].wait_recv()

        barrier = pltpu.get_barrier_semaphore()
        peers = [mate]
        peers += [at_y(d) for d in (1, 2, 3)]
        peers += [at_x(d) for d in (1, 2, 3)]
        peers += [at_z(d) for d in range(1, 8)]
        for p in peers:
            pl.semaphore_signal(barrier, 1, device_id=p, device_id_type=MESH)

        l_feat = load(1, feat_hbm, feat_v)
        l_cot = load(0, cot_hbm, cot_v)
        l_out = load(2, out_hbm, outw)
        l_in = load(3, in_hbm, inw)
        l_qkv = load(4, qkv_hbm, qkvw)

        count = count_ref[0]
        own_ids = view * own + lax.broadcasted_iota(jnp.int32, (own, 1), 0)
        live = jnp.where(own_ids < count, 1.0, 0.0).astype(F32)
        proj_row = proj_ref[pl.ds(view, 1), :]
        for kk in range(2):
            par = k if kk else 1 - k
            for d in range(4):
                ids = (
                    ((c + 4 - d) % 4) * (2 * own)
                    + par * own
                    + lax.broadcasted_iota(jnp.int32, (own, patches), 0)
                )
                hot[kk, own * d : own * (d + 1), :] = jnp.where(ids == proj_row, 1.0, 0.0).astype(BF16)

        mate_cp, relay_cp, y_cp = [], [], []

        def sums(j, kk):
            return dot_nn(hot[kk], feat_v[:, cols * j : cols * (j + 1)])

        def combine(j):
            mate_cp[j].wait_recv()
            both = pown[j] + precv[j].astype(F32)
            pown[j] = both
            far = slice(2 * own, 3 * own)
            ysend[j, far, :] = both[far, :].astype(BF16)
            relay_cp.append(
                [
                    send(
                        ysend.at[j, rows_of(2), pl.ds(cols // 2 * s, cols // 2)],
                        rrecv.at[s, j],
                        at_y((1, 3)[s]),
                    )
                    for s in range(2)
                ]
            )

        def forward(j):
            cps = []
            for s, d in ((0, 3), (1, 1)):
                relay_cp[j][s].wait_recv()
                block = pown[j, own * d : own * (d + 1), :]
                at = slice(own * d, own * (d + 1))
                mid = cols // 2
                passed = rrecv[s, j].astype(F32)
                if s == 0:
                    ysend[j, at, 0:mid] = (block[:, 0:mid] + passed).astype(BF16)
                    ysend[j, at, mid:] = block[:, mid:].astype(BF16)
                else:
                    ysend[j, at, 0:mid] = block[:, 0:mid].astype(BF16)
                    ysend[j, at, mid:] = (block[:, mid:] + passed).astype(BF16)
                cps.append(send(ysend.at[j, rows_of(d)], yrecv.at[s, j], at_y(4 - d)))
            y_cp.append(cps)

        l_feat.wait()
        psend[0] = sums(0, 0).astype(BF16)
        pl.semaphore_wait(barrier, len(peers))
        mate_cp.append(send(psend.at[0], precv.at[0], mate))
        l_cot.wait()
        seeds[0:own, :] = (cot_v[...].astype(F32) * live * (1.0 / objects)).astype(BF16)
        l_out.wait()
        for t in range(4):
            gsend[t] = dot_nt(seeds[0:own, :], outw[part * t : part * (t + 1), :]).astype(BF16)
        o_cp = [send(gsend.at[(c + d) % 4], gouts.at[rows_of(d)], at_y(d)) for d in (1, 2, 3)]
        gouts[0:own, :] = gsend[c]
        pown[0] = sums(0, 1)
        for j in range(1, CHUNKS):
            psend[j] = sums(j, 0).astype(BF16)
            mate_cp.append(send(psend.at[j], precv.at[j], mate))
            combine(j - 1)
            pown[j] = sums(j, 1)
            if j > 1:
                forward(j - 2)
        combine(CHUNKS - 1)
        forward(CHUNKS - 2)

        number = jnp.zeros((own, 1), F32)
        for w in range(views):
            same = proj_ref[w : w + 1, :] == view * own + lax.broadcasted_iota(
                jnp.int32, (own, patches), 0
            )
            number += jnp.sum(jnp.where(same, 1.0, 0.0), axis=1, keepdims=True)
        number = jnp.maximum(number, 1.0)
        forward(CHUNKS - 1)

        l_qkv.wait()
        for t in range(3):
            window = qkvw[:, pl.ds(pl.multiple_of(width * t + 128 * ((3 * c) // 2), 128), 256)]

            @pl.when(c % 2 == 0)
            def _():
                wown[:, part * t : part * (t + 1)] = window[:, 0:part]

            @pl.when(c % 2 == 1)
            def _():
                wown[:, part * t : part * (t + 1)] = window[:, 64 : 64 + part]

        for j in range(CHUNKS):
            total = pown[j, 0:own, :]
            for s in range(2):
                y_cp[j][s].wait_recv()
                total += yrecv[s, j].astype(F32)
            vox[:, cols * j : cols * (j + 1)] = (total / number).astype(BF16)
        l_in.wait()
        base_rows = dot_nn(vox[...], inw[...])
        base[...] = base_rows
        shifted = base_rows - jnp.mean(base_rows, axis=1, keepdims=True)
        spread = jnp.mean(shifted * shifted, axis=1, keepdims=True)
        inverse = lax.rsqrt(spread + 1e-06)
        unit_rows = shifted * inverse
        unit[...] = unit_rows
        gain = gain_ref[...].reshape(1, width)
        normed[0:own, :] = (unit_rows * gain).astype(BF16)
        n_cp = gather_start(normed)

        kv_cp = []

        def project(d):
            at = slice(own * d, own * (d + 1))
            packed = dot_nn(normed[at, :], wown[...])
            qs[at, :] = (packed[:, 0:part] * (HEAD_DIM**-0.5)).astype(BF16)
            kvs[at, :] = packed[:, part : 3 * part].astype(BF16)
            kv_cp.append(
                send(kvs.at[rows_of(d)], kvs.at[pl.ds(group + own * d, own)], mate)
            )
            turned[:, at] = normed[at, :].T

        project(0)
        gather_pass(normed, n_cp)
        s_cp = gather_start(seeds)
        for d in (1, 3):
            gather_wait(n_cp, d)
            project(d)
        gather_wait(n_cp, 2)
        project(2)
        gather_pass(seeds, s_cp)
        v_cp = [
            send(
                vox.at[:, pl.ds(pl.multiple_of(vcols * ((c + d) % 4), 128), vcols)],
                vcol.at[rows_of(d)],
                at_y(d),
            )
            for d in (1, 2, 3)
        ]
        vcol[0:own, :] = vox[:, pl.ds(pl.multiple_of(vcols * c, 128), vcols)]

        lane = lax.broadcasted_iota(jnp.int32, (1, own), 1)
        pieces = []
        for par in (k, 1 - k):
            for d in range(4):
                ids = ((c + 4 - d) % 4) * (2 * own) + par * own + lane
                pieces.append(jnp.where(ids < count, 0.0, NEG).astype(F32))
        bias = jnp.concatenate(pieces, axis=1)
        for cp in kv_cp:
            cp.wait_recv()
        for cp in o_cp:
            cp.wait_recv()

        dkv_cp, g_cp, qg_cp, t_cp = [], [], [], []

        def attend(h):
            hs = slice(HEAD_DIM * h, HEAD_DIM * (h + 1))
            keys = kvs[:, hs]
            values = kvs[:, part + HEAD_DIM * h : part + HEAD_DIM * (h + 1)]
            grad_k = jnp.zeros((slots, HEAD_DIM), F32)
            grad_v = jnp.zeros((slots, HEAD_DIM), F32)
            for b in range(group // QROWS):
                rs = slice(QROWS * b, QROWS * (b + 1))
                q = qs[rs, hs]
                go = gouts[rs, hs]
                s = dot_nt(q, keys) + bias
                e = jnp.exp(s - jnp.max(s, axis=1, keepdims=True))
                w = e * (1.0 / jnp.sum(e, axis=1, keepdims=True))
                p = w.astype(BF16)
                mixed = dot_nn(p, values)
                att[rs, hs] = mixed.astype(BF16)
                delta = jnp.sum(go.astype(F32) * mixed, axis=1, keepdims=True)
                gs = (w * (dot_nt(go, values) - delta)).astype(BF16)
                gp[h, rs, 0:HEAD_DIM] = (dot_nn(gs, keys) * (HEAD_DIM**-0.5)).astype(BF16)
                grad_k += dot_tn(gs, q)
                grad_v += dot_tn(p, go)
            both = jnp.concatenate([grad_k, grad_v], axis=1)
            dkv_send[h] = both[group:].astype(BF16)
            dkv_cp.append(send(dkv_send.at[h], dkv_recv.at[h], mate))
            dkv[h] = both[0:group]

        def finish(h):
            dkv_cp[h].wait_recv()
            both = dkv[h] + dkv_recv[h].astype(F32)
            gp[h, :, HEAD_DIM:] = both.astype(BF16)
            for d in (2, 1, 3):
                g_cp.append(send(gp.at[h, rows_of(d)], gpr.at[c, h], at_y(4 - d)))
            gpr[c, h] = gp[h, 0:own, :]
            whole = dot_nn(turned[...], gp[h])
            for t in range(8):
                qg[h, t] = whole[orows * t : orows * (t + 1), :]
            for t in range(4):
                qg_send[h, t] = qg[h, 2 * t + (1 - k)].astype(BF16)
            qg_cp.append(send(qg_send.at[h], qg_recv.at[h], mate))

        def swap(h):
            qg_cp[h].wait_recv()
            for t in range(4):
                qsum[h, t] = (qg[h, 2 * t + k] + qg_recv[h, t].astype(F32)).astype(BF16)
            for d in (2, 1, 3):
                t_cp.append(send(qsum.at[h, (c + d) % 4], qrecv.at[c, h], at_y(d)))
            qrecv[c, h] = qsum[h, c]

        attend(0)
        attend(1)
        finish(0)
        attend(2)
        finish(1)
        swap(0)
        for d in (1, 3, 2):
            gather_wait(s_cp, d)
        og[...] = dot_tn(att[...], seeds[...])
        og_send[...] = og[pl.ds(pl.multiple_of(orows * (1 - k), 32), orows), :].astype(BF16)
        og_cp = send(og_send, og_recv, mate)
        finish(2)
        swap(1)
        swap(2)
        a_cp = [send(att.at[rows_of(d)], attr.at[c], at_y(4 - d)) for d in (1, 2, 3)]
        attr[c] = att[0:own, :]

        og_cp.wait_recv()
        og_sum = (
            og[pl.ds(pl.multiple_of(orows * k, 32), orows), :] + og_recv[...].astype(F32)
        ).astype(BF16)
        for r in range(4):
            mx[3, r] = og_sum[24 * r : 24 * (r + 1), :]

        for cp in g_cp:
            cp.wait_recv()
        for t in range(4):
            for h in range(3):
                for s3 in range(3):
                    at = width * s3 + part * t + HEAD_DIM * h
                    gpfull[:, at : at + HEAD_DIM] = gpr[
                        t, h, :, HEAD_DIM * s3 : HEAD_DIM * (s3 + 1)
                    ]
        grad_unit = dot_nt(gpfull[...], qkvw[...]) * gain
        unit_rows = unit[...]
        branch_grad = inverse * (
            grad_unit
            - jnp.mean(grad_unit, axis=1, keepdims=True)
            - unit_rows * jnp.mean(grad_unit * unit_rows, axis=1, keepdims=True)
        )
        gball[0:own, :] = (seeds[0:own, :].astype(F32) + branch_grad).astype(BF16)
        b_cp = gather_start(gball)

        for cp in t_cp:
            cp.wait_recv()
        for s3 in range(3):
            for t in range(4):
                for h in range(3):
                    at = part * t + HEAD_DIM * h
                    joined[s3, :, at : at + HEAD_DIM] = qrecv[
                        t, h, :, HEAD_DIM * s3 : HEAD_DIM * (s3 + 1)
                    ]
            for r in range(4):
                mx[s3, r] = joined[s3, 24 * r : 24 * (r + 1), :]

        def x_scatter(buf, recv):
            return [send(buf.at[(x + d) % 4], recv.at[d - 1], at_x(d)) for d in (2, 1, 3)]

        def x_sum(buf, recv, cps, out):
            for cp in cps:
                cp.wait_recv()
            out[...] = (
                buf[x].astype(F32)
                + recv[0].astype(F32)
                + recv[1].astype(F32)
                + recv[2].astype(F32)
            ).astype(BF16)

        half = width // 2
        z_order = (4, 3, 5, 2, 6, 1, 7)

        def z_piece(buf, where):
            return buf.at[where // 2, :, pl.ds(pl.multiple_of(half * (where % 2), 128), half)]

        def z_scatter(buf, recv):
            return [send(z_piece(buf, (z + d) % 8), recv.at[d - 1], at_z(d)) for d in z_order]

        def z_sum(buf, recv, cps, out):
            total = z_piece(buf, z)[...].astype(F32)
            for cp in cps:
                cp.wait_recv()
            for d in range(1, 8):
                total += recv[d - 1].astype(F32)
            out[...] = total.astype(BF16)

        def z_gather(fin, full):
            cps = [send(fin, z_piece(full.at[x], z), at_z(d)) for d in z_order]
            full[x, z // 2, :, pl.ds(pl.multiple_of(half * (z % 2), 128), half)] = fin[...]
            return cps

        def x_gather(full, cps):
            for cp in cps:
                cp.wait_recv()
            return [send(full.at[x], full.at[x], at_x(d)) for d in (2, 1, 3)]

        mx_cp = x_scatter(mx, mxr)
        gather_pass(gball, b_cp)
        for cp in a_cp:
            cp.wait_recv()
        for t in range(4):
            afull[:, part * t : part * (t + 1)] = attr[t]
        branch = dot_nn(afull[...], outw[...])
        latent_ref[...] = (live * (base[...] + branch)).astype(BF16)

        for cp in v_cp:
            cp.wait_recv()
        for d in (1, 3, 2):
            gather_wait(b_cp, d)
        ig[...] = dot_tn(vcol[...], gball[...])
        ig_send[...] = ig[pl.ds(pl.multiple_of(own * (1 - k), 128), own), :].astype(BF16)
        ig_cp = send(ig_send, ig_recv, mate)
        x_sum(mx, mxr, mx_cp, mz)
        mz_cp = z_scatter(mz, mzr)
        ig_cp.wait_recv()
        ig_sum = (
            ig[pl.ds(pl.multiple_of(own * k, 128), own), :] + ig_recv[...].astype(F32)
        ).astype(BF16)
        for t in range(4):
            for r in range(4):
                ix[t, r] = ig_sum[32 * t + 8 * r : 32 * t + 8 * (r + 1), :]
        ix_cp = x_scatter(ix, ixr)

        x_sum(ix, ixr, ix_cp, iz)
        iz_cp = z_scatter(iz, izr)
        z_sum(mz, mzr, mz_cp, mf)
        mg_cp = z_gather(mf, mg)
        z_sum(iz, izr, iz_cp, jf)
        jg_cp = z_gather(jf, jg)
        mo_cp = x_gather(mg, mg_cp)
        jo_cp = x_gather(jg, jg_cp)
        for cp in mo_cp:
            cp.wait_recv()
        gmain_ref[...] = mg[...]
        for cp in jo_cp:
            cp.wait_recv()
        gin_ref[...] = jg[...]
        for cp in sent:
            cp.wait_send()

    scratch = [
        ((patches, feat), BF16), ((feat, width), BF16), ((width, 3 * width), BF16),
        ((width, width), BF16), ((own, width), BF16), ((2, group, patches), BF16),
        ((CHUNKS, group, cols), BF16), ((CHUNKS, group, cols), BF16), ((CHUNKS, group, cols), F32),
        ((CHUNKS, group, cols), BF16), ((2, CHUNKS, own, cols // 2), BF16),
        ((2, CHUNKS, own, cols), BF16),
        ((group, width), BF16), ((own, feat), BF16), ((group, vcols), BF16),
        ((own, width), F32), ((own, width), F32), ((group, width), BF16), ((width, group), BF16),
        ((width, 3 * part), BF16), ((group, part), BF16), ((slots, 2 * part), BF16),
        ((4, own, part), BF16), ((group, part), BF16), ((group, part), BF16),
        ((4, own, part), BF16), ((own, width), BF16),
        ((heads, group, 128), F32), ((heads, group, 128), BF16), ((heads, group, 128), BF16),
        ((heads, group, part), BF16), ((4, heads, own, part), BF16), ((own, 3 * width), BF16),
        ((part, width), F32), ((orows, width), BF16), ((orows, width), BF16),
        ((heads, 8, orows, part), F32), ((heads, 4, orows, part), BF16),
        ((heads, 4, orows, part), BF16), ((heads, 4, orows, part), BF16),
        ((4, heads, orows, part), BF16), ((3, orows, width), BF16),
        ((group, width), BF16), ((2 * own, width), F32), ((own, width), BF16), ((own, width), BF16),
        ((4, 4, 24, width), BF16), ((3, 4, 24, width), BF16), ((4, 24, width), BF16),
        ((7, 24, width // 2), BF16), ((24, width // 2), BF16), ((4, 4, 24, width), BF16),
        ((4, 4, 8, width), BF16), ((3, 4, 8, width), BF16), ((4, 8, width), BF16),
        ((7, 8, width // 2), BF16), ((8, width // 2), BF16), ((4, 4, 8, width), BF16),
    ]
    return kernel, scratch


def write_out(latent_ref, gin_ref, gmain_ref, latent_out, in_out, qkv_out, out_out):
    width = latent_ref.shape[1]
    latent_out[...] = latent_ref[...]
    for t in range(4):
        for r in range(4):
            at = slice(32 * t + 8 * r, 32 * t + 8 * (r + 1))
            in_out[at, :] = gin_ref[t, r].astype(F32)
    for r in range(4):
        at = slice(24 * r, 24 * (r + 1))
        for s in range(3):
            qkv_out[at, width * s : width * (s + 1)] = gmain_ref[s, r].astype(F32)
        out_out[at, :] = gmain_ref[3, r].astype(F32)


def per_device(
    features, projection, active_count, in_weight, norm_gain, qkv_weight, out_weight, cotangent
):
    patches, feat = features.shape[2:]
    own, width = cotangent.shape[1:]
    views = projection.shape[1]
    objects = lax.axis_size("obj")
    kernel, scratch = make_kernel((patches, feat, width, own, objects, views))
    vmem = pl.BlockSpec(memory_space=pltpu.VMEM)
    hbm = pl.BlockSpec(memory_space=pl.ANY)
    latent, gin, gmain = pl.pallas_call(
        kernel,
        name="encode",
        out_shape=(
            jax.ShapeDtypeStruct((own, width), BF16),
            jax.ShapeDtypeStruct((4, 4, 8, width), BF16),
            jax.ShapeDtypeStruct((4, 4, 24, width), BF16),
        ),
        in_specs=[hbm, vmem, pl.BlockSpec(memory_space=pltpu.SMEM), hbm, vmem, hbm, hbm, hbm],
        out_specs=(vmem, vmem, vmem),
        scratch_shapes=[pltpu.VMEM(s, t) for s, t in scratch]
        + [
            pltpu.SemaphoreType.DMA((128,)),
            pltpu.SemaphoreType.DMA((128,)),
            pltpu.SemaphoreType.DMA((5,)),
        ],
        compiler_params=pltpu.CompilerParams(
            collective_id=0, has_side_effects=True, vmem_limit_bytes=62 * 1024 * 1024
        ),
    )(
        features.reshape(patches, feat),
        projection.reshape(views, patches),
        active_count,
        in_weight,
        norm_gain,
        qkv_weight,
        out_weight,
        cotangent.reshape(own, width),
    )
    latent, in_grad, qkv_grad, out_grad = pl.pallas_call(
        write_out,
        name="write_out",
        out_shape=(
            jax.ShapeDtypeStruct((own, width), BF16),
            jax.ShapeDtypeStruct((own, width), F32),
            jax.ShapeDtypeStruct((96, 3 * width), F32),
            jax.ShapeDtypeStruct((96, width), F32),
        ),
        in_specs=[vmem, vmem, vmem],
        out_specs=(vmem, vmem, vmem, vmem),
    )(latent, gin, gmain)
    return (latent[None], in_grad, qkv_grad, out_grad)


def solution(mesh):
    return jax.shard_map(
        per_device,
        mesh=mesh,
        in_specs=(
            P("obj", "view", None, None),
            P("obj", None, None),
            P("obj"),
            P(),
            P(),
            P(),
            P(),
            P("obj", "view", None),
        ),
        out_specs=(P("obj", "view", None), P("view", None), P("view", None), P("view", None)),
        check_vma=False,
    )
```

time: 116 us -> 104 us (0.90)
  Pallas kernels: 108 us -> 103 us
  local copies, waits for them, and re-layouts: 3.17 us -> 0 us
  other arithmetic: 2.5 us -> 0 us
    pallas_call x1, Pallas kernels: 108 us -> 100 us  [per_device(): pl.pallas_call(kernel, name='encode', out_shape=(jax.ShapeDtypeStruct((ow...]
    pallas_call x0 -> x1, Pallas kernels: none -> 2.5 us  [per_device(): pl.pallas_call(write_out, name='write_out', out_shape=(jax.ShapeDtypeStru...]
    convert_element_type x3 -> x0, other arithmetic: 2.5 us -> none  [the longest x1 0.97 us: per_device(): jnp.concatenate([gmain[0], gmain[1], gmain[2]], axis=1).astype(F32)]
    reshape x1 -> x0, local copies, waits for them, and re-layouts: 1.27 us -> none  [per_device(): norm_gain.reshape(1, width)]
    slice x1 -> x0, local copies, waits for them, and re-layouts: 1.21 us -> none  [per_device(): gmain[3].astype(F32)]
where the time goes in v2:
time: 104 us
  Pallas kernels  103 us (99%)
  between operations  1.29 us (1%)
    pallas_call x1, Pallas kernels, per_device(): pl.pallas_call(kernel, name='encode', out_shape=(jax.ShapeDtypeStruct((ow...  100 us
    pallas_call x1, Pallas kernels, per_device(): pl.pallas_call(write_out, name='write_out', out_shape=(jax.ShapeDtypeStru...  2.5 us

profile of v2, /device:TPU:1, one launch (start us, length us, event | category | flops | bytes accessed | tf_op | source)
XLA Modules:
  0.0 104.0 jit_solution(1299898105765533597)
XLA Ops:
  1.3 100.2 %encode.1 = (bf16[128,768]{1,0:T(8,128)(2,1)}, bf16[4,4,8,768]{3,2,1,0:T(8,128)(2,1)}, bf16[4,4,24,768]{3,2,1,0:T(8,128)(2,1)}) custom-call(bf16[1369,1024]{1,0:T(8,128)(2,1)} %bitcast.4, s32[8,1369]{1,0:T(8,128)} %bitcast.6, s32[1]{0:T(128)S(6)} %copy.12.count_ref, bf16[1024,768]{1,0:T(8,128)(2,1)} %in_hbm.1, f32[768]{0:T(1024)} %gain_ref.1, ...), custom_call_target="tpu_custom_call" | custom-call | tf_op jit(solution)/shard_map/encode/pallas_call | solution.py:520
  101.5 2.5 %write_out.1 = (bf16[128,768]{1,0:T(8,128)(2,1)}, f32[128,768]{1,0:T(8,128)}, f32[96,2304]{1,0:T(8,128)}, f32[96,768]{1,0:T(8,128)}) custom-call(bf16[128,768]{1,0:T(8,128)(2,1)} %get-tuple-element.11.latent_ref, bf16[4,4,8,768]{3,2,1,0:T(8,128)(2,1)} %get-tuple-element.12.gin_ref, bf16[4,4,24,768]{3,2,1,0:T(8,128)(2,1)} %get-tuple-element.13.gmain_ref), custom_call_target="tpu_custom_call" | custom-call | tf_op jit(solution)/shard_map/write_out/pallas_call | solution.py:549

commit v3 on v2

v3 whole, which is shorter than its diff:
```python
import jax
import jax.numpy as jnp
from jax import lax
from jax.experimental import pallas as pl
from jax.experimental.pallas import tpu as pltpu
from jax.sharding import PartitionSpec as P

HEAD_DIM = 64
MESH = pl.DeviceIdType.MESH
F32 = jnp.float32
BF16 = jnp.bfloat16
NEG = -1e30
CHUNKS = 4
QROWS = 256


def dot_nn(a, b):
    return lax.dot_general(a, b, (((1,), (0,)), ((), ())), preferred_element_type=F32)


def dot_nt(a, b):
    return lax.dot_general(a, b, (((1,), (1,)), ((), ())), preferred_element_type=F32)


def dot_tn(a, b):
    return lax.dot_general(a, b, (((0,), (0,)), ((), ())), preferred_element_type=F32)


class Group:
    def __init__(self, like, send_sem, recv_sem):
        self.like, self.send_sem, self.recv_sem = like, send_sem, recv_sem

    def wait_send(self):
        pltpu.make_async_copy(self.like, self.like, self.send_sem).wait()

    def wait_recv(self):
        pltpu.make_async_copy(self.like, self.like, self.recv_sem).wait()


def make_kernel(sizes):
    patches, feat, width, own, objects, views = sizes
    chips = 4
    heads = 3
    part = heads * HEAD_DIM
    group = chips * own
    slots = 2 * group
    cols = feat // CHUNKS
    vcols = feat // chips
    orows = part // 2

    def kernel(
        feat_hbm, proj_hbm, count_hbm, in_hbm, gain_hbm, qkv_hbm, out_hbm, cot_hbm,
        latent_hbm, gin_hbm, gmain_hbm,
        proj_ref, gain_ref, latent_v, feat_v, inw, qkvw, outw, cot_v, hot, psend, precv, pown, ysend, rrecv, yrecv,
        seeds, vox, vcol, base, unit, normed, turned, wown, qs, kvs, gsend, gouts, att, afull,
        dkv, dkv_send, dkv_recv, gp, gq, gpr, gpfull, og, og_send, og_recv,
        qg, qg_send, qg_recv, qsum, qlast, qrecv, qrlast, gball, ig, ig_send, ig_recv,
        mx, mxr, mz, mzr, mf, mg, ix, ixr, jf, jg,
        count_ref, ssem, rsem, lsem, ready,
    ):
        obj = lax.axis_index("obj")
        view = lax.axis_index("view")
        c = view // 2
        k = view % 2
        z = obj // 4
        x = obj % 4

        def at_y(d):
            return (obj, ((c + d) % 4) * 2 + k)

        def at_x(d):
            return (z * 4 + (x + d) % 4, view)

        def at_z(d):
            return (((z + d) % 8) * 4 + x, view)

        def at_o(dz, dx):
            return (((z + dz) % 8) * 4 + (x + dx) % 4, view)

        others = [(dz, dx) for dz in (4, 3, 5, 2, 6, 1, 7, 0) for dx in (2, 1, 3, 0) if dz or dx]
        mate = (obj, c * 2 + (1 - k))
        used = [0]
        sent = []

        def send(src, dst, device):
            n = used[0]
            used[0] += 1
            cp = pltpu.make_async_remote_copy(
                src_ref=src, dst_ref=dst, send_sem=ssem.at[n], recv_sem=rsem.at[n],
                device_id=device, device_id_type=MESH,
            )
            cp.start()
            sent.append(cp)
            return cp

        def send_all(triples, like):
            n = used[0]
            used[0] += 1
            for src, dst, device in triples:
                pltpu.make_async_remote_copy(
                    src_ref=src, dst_ref=dst, send_sem=ssem.at[n], recv_sem=rsem.at[n],
                    device_id=device, device_id_type=MESH,
                ).start()
            group = Group(like, ssem.at[n], rsem.at[n])
            sent.append(group)
            return group

        def load(n, src, dst):
            cp = pltpu.make_async_copy(src, dst, lsem.at[n])
            cp.start()
            return cp

        def rows_of(d, half=None):
            if half is None:
                return pl.ds(own * d, own)
            return pl.ds(own * d + own // 2 * half, own // 2)

        def gather_start(buf):
            out = {}
            for to, slot, order in ((1, 1, (0, 1)), (3, 3, (1, 0))):
                for half in order:
                    out[slot, half] = send(
                        buf.at[rows_of(0, half)], buf.at[rows_of(slot, half)], at_y(to)
                    )
            return out

        def gather_pass(buf, cps):
            cps[1, 0].wait_recv()
            cps[2, 0] = send(buf.at[rows_of(1, 0)], buf.at[rows_of(2, 0)], at_y(1))
            cps[3, 1].wait_recv()
            cps[2, 1] = send(buf.at[rows_of(3, 1)], buf.at[rows_of(2, 1)], at_y(3))

        def gather_wait(cps, slot):
            for half in ((1,), (0, 1), (0,))[slot - 1]:
                cps[slot, half].wait_recv()

        barrier = pltpu.get_barrier_semaphore()
        peers = [mate]
        peers += [at_y(d) for d in (1, 2, 3)]
        peers += [at_x(d) for d in (1, 2, 3)]
        peers += [at_z(d) for d in range(1, 8)]
        for p in peers:
            pl.semaphore_signal(barrier, 1, device_id=p, device_id_type=MESH)

        l_proj = load(5, proj_hbm, proj_ref)
        l_count = load(6, count_hbm, count_ref)
        l_cot = load(0, cot_hbm, cot_v)
        l_feat = [
            load(10 + j, feat_hbm.at[:, pl.ds(cols * j, cols)], feat_v.at[j]) for j in range(CHUNKS)
        ]
        l_out = load(2, out_hbm, outw)
        l_in = load(3, in_hbm, inw)
        l_gain = load(7, gain_hbm, gain_ref)
        l_qkv = load(4, qkv_hbm, qkvw)

        l_proj.wait()
        l_count.wait()
        count = count_ref[0]
        own_ids = view * own + lax.broadcasted_iota(jnp.int32, (own, 1), 0)
        live = jnp.where(own_ids < count, 1.0, 0.0).astype(F32)
        proj_row = proj_ref[pl.ds(view, 1), :]
        for kk in range(2):
            par = k if kk else 1 - k
            for d in range(4):
                ids = (
                    ((c + 4 - d) % 4) * (2 * own)
                    + par * own
                    + lax.broadcasted_iota(jnp.int32, (own, patches), 0)
                )
                hot[kk, own * d : own * (d + 1), :] = jnp.where(ids == proj_row, 1.0, 0.0).astype(BF16)

        mate_cp, relay_cp, y_cp = [], [], []

        def sums(j, kk):
            return dot_nn(hot[kk], feat_v[j])

        def combine(j):
            mate_cp[j].wait_recv()
            both = pown[j] + precv[j].astype(F32)
            pown[j] = both
            far = slice(2 * own, 3 * own)
            ysend[j, far, :] = both[far, :].astype(BF16)
            relay_cp.append(
                send_all(
                    [
                        (
                            ysend.at[j, rows_of(2), pl.ds(cols // 2 * s, cols // 2)],
                            rrecv.at[j, s],
                            at_y((1, 3)[s]),
                        )
                        for s in range(2)
                    ],
                    rrecv.at[j],
                )
            )

        def forward(j):
            relay_cp[j].wait_recv()
            mid = cols // 2
            for s, d in ((0, 3), (1, 1)):
                at = slice(own * d, own * (d + 1))
                block = pown[j, at, :]
                passed = rrecv[j, s].astype(F32)
                if s == 0:
                    ysend[j, at, 0:mid] = (block[:, 0:mid] + passed).astype(BF16)
                    ysend[j, at, mid:] = block[:, mid:].astype(BF16)
                else:
                    ysend[j, at, 0:mid] = block[:, 0:mid].astype(BF16)
                    ysend[j, at, mid:] = (block[:, mid:] + passed).astype(BF16)
            y_cp.append(
                send_all(
                    [
                        (ysend.at[j, rows_of(d)], yrecv.at[j, s], at_y(4 - d))
                        for s, d in ((0, 3), (1, 1))
                    ],
                    yrecv.at[j],
                )
            )

        l_cot.wait()
        seeds[0:own, :] = (cot_v[...].astype(F32) * live * (1.0 / objects)).astype(BF16)
        l_feat[0].wait()
        psend[0] = sums(0, 0).astype(BF16)
        pl.semaphore_wait(barrier, len(peers))
        mate_cp.append(send(psend.at[0], precv.at[0], mate))
        for p in range(1, 4):
            pl.semaphore_signal(ready, 1, device_id=at_x(p), device_id_type=MESH)
        l_out.wait()
        for t in range(4):
            gsend[t] = dot_nt(seeds[0:own, :], outw[part * t : part * (t + 1), :]).astype(BF16)
        o_cp = send_all(
            [(gsend.at[(c + d) % 4], gouts.at[rows_of(d)], at_y(d)) for d in (2, 1, 3)],
            gouts.at[pl.ds(0, 3 * own)],
        )
        gouts[0:own, :] = gsend[c]
        pown[0] = sums(0, 1)
        for j in range(1, CHUNKS):
            l_feat[j].wait()
            psend[j] = sums(j, 0).astype(BF16)
            mate_cp.append(send(psend.at[j], precv.at[j], mate))
            combine(j - 1)
            pown[j] = sums(j, 1)
            if j > 1:
                forward(j - 2)
        combine(CHUNKS - 1)
        forward(CHUNKS - 2)

        number = jnp.zeros((own, 1), F32)
        for w in range(views):
            same = proj_ref[w : w + 1, :] == view * own + lax.broadcasted_iota(
                jnp.int32, (own, patches), 0
            )
            number += jnp.sum(jnp.where(same, 1.0, 0.0), axis=1, keepdims=True)
        number = jnp.maximum(number, 1.0)
        forward(CHUNKS - 1)

        l_qkv.wait()
        for t in range(3):
            window = qkvw[:, pl.ds(pl.multiple_of(width * t + 128 * ((3 * c) // 2), 128), 256)]

            @pl.when(c % 2 == 0)
            def _():
                wown[:, part * t : part * (t + 1)] = window[:, 0:part]

            @pl.when(c % 2 == 1)
            def _():
                wown[:, part * t : part * (t + 1)] = window[:, 64 : 64 + part]

        for j in range(CHUNKS):
            total = pown[j, 0:own, :]
            y_cp[j].wait_recv()
            total += yrecv[j, 0].astype(F32) + yrecv[j, 1].astype(F32)
            vox[:, cols * j : cols * (j + 1)] = (total / number).astype(BF16)
        l_in.wait()
        base_rows = dot_nn(vox[...], inw[...])
        base[...] = base_rows
        shifted = base_rows - jnp.mean(base_rows, axis=1, keepdims=True)
        spread = jnp.mean(shifted * shifted, axis=1, keepdims=True)
        inverse = lax.rsqrt(spread + 1e-06)
        unit_rows = shifted * inverse
        unit[...] = unit_rows
        l_gain.wait()
        gain = gain_ref[...].reshape(1, width)
        normed[0:own, :] = (unit_rows * gain).astype(BF16)
        n_cp = gather_start(normed)

        kv_n = used[0]
        used[0] += 1

        def share(d):
            pltpu.make_async_remote_copy(
                src_ref=kvs.at[rows_of(d)], dst_ref=kvs.at[pl.ds(group + own * d, own)],
                send_sem=ssem.at[kv_n], recv_sem=rsem.at[kv_n],
                device_id=mate, device_id_type=MESH,
            ).start()

        kv_cp = Group(kvs.at[pl.ds(0, group)], ssem.at[kv_n], rsem.at[kv_n])
        sent.append(kv_cp)

        def project(d):
            at = slice(own * d, own * (d + 1))
            packed = dot_nn(normed[at, :], wown[...])
            qs[at, :] = (packed[:, 0:part] * (HEAD_DIM**-0.5)).astype(BF16)
            kvs[at, :] = packed[:, part : 3 * part].astype(BF16)
            share(d)
            turned[:, at] = normed[at, :].T

        project(0)
        gather_pass(normed, n_cp)
        for d in (1, 3):
            gather_wait(n_cp, d)
            project(d)
        gather_wait(n_cp, 2)
        project(2)
        s_cp = gather_start(seeds)

        lane = lax.broadcasted_iota(jnp.int32, (1, own), 1)
        pieces = []
        for par in (k, 1 - k):
            for d in range(4):
                ids = ((c + 4 - d) % 4) * (2 * own) + par * own + lane
                pieces.append(jnp.where(ids < count, 0.0, NEG).astype(F32))
        bias = jnp.concatenate(pieces, axis=1)
        kv_cp.wait_recv()
        o_cp.wait_recv()

        dkv_cp, g_cp, qg_cp, t_cp = [], [], [], []

        def attend(h):
            hs = slice(HEAD_DIM * h, HEAD_DIM * (h + 1))
            keys = kvs[:, hs]
            values = kvs[:, part + HEAD_DIM * h : part + HEAD_DIM * (h + 1)]
            grad_k = jnp.zeros((slots, HEAD_DIM), F32)
            grad_v = jnp.zeros((slots, HEAD_DIM), F32)
            for b in range(group // QROWS):
                rs = slice(QROWS * b, QROWS * (b + 1))
                q = qs[rs, hs]
                go = gouts[rs, hs]
                s = dot_nt(q, keys) + bias
                e = jnp.exp(s - jnp.max(s, axis=1, keepdims=True))
                w = e * (1.0 / jnp.sum(e, axis=1, keepdims=True))
                p = w.astype(BF16)
                mixed = dot_nn(p, values)
                att[rs, hs] = mixed.astype(BF16)
                delta = jnp.sum(go.astype(F32) * mixed, axis=1, keepdims=True)
                gs = (w * (dot_nt(go, values) - delta)).astype(BF16)
                grad_q = (dot_nn(gs, keys) * (HEAD_DIM**-0.5)).astype(BF16)
                gq[h, rs, 0:HEAD_DIM] = grad_q
                gp[h, rs, 0:128] = jnp.concatenate([grad_q, mixed.astype(BF16)], axis=1)
                grad_k += dot_tn(gs, q)
                grad_v += dot_tn(p, go)
            both = jnp.concatenate([grad_k, grad_v], axis=1)
            dkv_send[h] = both[group:].astype(BF16)
            dkv_cp.append(send(dkv_send.at[h], dkv_recv.at[h], mate))
            dkv[h] = both[0:group]

        def finish(h):
            dkv_cp[h].wait_recv()
            both = dkv[h] + dkv_recv[h].astype(F32)
            both = both.astype(BF16)
            gp[h, :, 128:] = both
            gq[h, :, HEAD_DIM:] = both
            g_cp.append(
                send_all(
                    [(gp.at[h, rows_of(d)], gpr.at[c, h], at_y(4 - d)) for d in (2, 1, 3)],
                    gp.at[h, pl.ds(0, 3 * own)],
                )
            )
            gpr[c, h] = gp[h, 0:own, :]
            whole = dot_nn(turned[...], gq[h])
            for t in range(8):
                qg[h, t] = whole[orows * t : orows * (t + 1), :]
            for t in range(4):
                qg_send[h, t] = qg[h, 2 * t + (1 - k)].astype(BF16)
            qg_cp.append(send(qg_send.at[h], qg_recv.at[h], mate))

        def swap(h):
            qg_cp[h].wait_recv()
            for t in range(4):
                block = (qg[h, 2 * t + k] + qg_recv[h, t].astype(F32)).astype(BF16)
                if h < 2:
                    qsum[t, :, part * h : part * (h + 1)] = block
                else:
                    qlast[t] = block
            if h:
                buf, recv = (qsum, qrecv) if h == 1 else (qlast, qrlast)
                t_cp.append(
                    send_all(
                        [(buf.at[(c + d) % 4], recv.at[c], at_y(d)) for d in (2, 1, 3)],
                        recv.at[pl.ds(0, 3)],
                    )
                )
                recv[c] = buf[c]

        def x_scatter(h):
            return send_all(
                [(mx.at[h, (x + d) % 4], mxr.at[h, d - 1], at_x(d)) for d in (2, 1, 3)],
                mxr.at[h],
            )

        def join(h):
            for t in range(4):
                for r in range(4):
                    rows = slice(24 * r, 24 * (r + 1))
                    if h < 2:
                        block = qrecv[t, rows, part * h : part * (h + 1)]
                    else:
                        block = qrlast[t, rows, :]
                    mx[h, r, :, part * t : part * (t + 1)] = block
            mx_cp.append(x_scatter(h))

        def place(h):
            g_cp[h].wait_recv()
            for t in range(4):
                for s3, lo in ((0, 0), (1, 128), (2, 192)):
                    at = width * s3 + part * t + HEAD_DIM * h
                    gpfull[:, at : at + HEAD_DIM] = gpr[t, h, :, lo : lo + HEAD_DIM]
                at = part * t + HEAD_DIM * h
                afull[:, at : at + HEAD_DIM] = gpr[t, h, :, HEAD_DIM : 2 * HEAD_DIM]

        attend(0)
        gather_pass(seeds, s_cp)
        v_cp = send_all(
            [
                (
                    vox.at[:, pl.ds(pl.multiple_of(vcols * ((c + d) % 4), 128), vcols)],
                    vcol.at[rows_of(d)],
                    at_y(d),
                )
                for d in (1, 2, 3)
            ],
            vcol.at[pl.ds(0, 3 * own)],
        )
        vcol[0:own, :] = vox[:, pl.ds(pl.multiple_of(vcols * c, 128), vcols)]
        attend(1)
        finish(0)
        attend(2)
        finish(1)
        swap(0)
        for d in (1, 3, 2):
            gather_wait(s_cp, d)
        og[...] = dot_tn(att[...], seeds[...])
        og_send[...] = og[pl.ds(pl.multiple_of(orows * (1 - k), 32), orows), :].astype(BF16)
        og_cp = send(og_send, og_recv, mate)
        finish(2)
        swap(1)
        swap(2)
        place(0)
        place(1)
        og_cp.wait_recv()
        og_sum = (
            og[pl.ds(pl.multiple_of(orows * k, 32), orows), :] + og_recv[...].astype(F32)
        ).astype(BF16)
        for r in range(4):
            mx[3, r] = og_sum[24 * r : 24 * (r + 1), :]
        mx_cp = [x_scatter(3)]
        place(2)
        grad_unit = dot_nt(gpfull[...], qkvw[...]) * gain
        unit_rows = unit[...]
        branch_grad = inverse * (
            grad_unit
            - jnp.mean(grad_unit, axis=1, keepdims=True)
            - unit_rows * jnp.mean(grad_unit * unit_rows, axis=1, keepdims=True)
        )
        gball[0:own, :] = (seeds[0:own, :].astype(F32) + branch_grad).astype(BF16)
        b_cp = gather_start(gball)

        t_cp[0].wait_recv()
        join(0)
        join(1)
        t_cp[1].wait_recv()
        join(2)

        half = width // 2
        z_order = (4, 3, 5, 2, 6, 1, 7)

        def z_piece(buf, where):
            return buf.at[where // 2, :, pl.ds(pl.multiple_of(half * (where % 2), 128), half)]

        gather_pass(gball, b_cp)
        branch = dot_nn(afull[...], outw[...])
        latent_v[...] = (live * (base[...] + branch)).astype(BF16)
        l_latent = load(8, latent_v, latent_hbm)

        for cp in mx_cp:
            cp.wait_recv()
        for h in range(4):
            mz[h] = (
                mx[h, x].astype(F32)
                + mxr[h, 0].astype(F32)
                + mxr[h, 1].astype(F32)
                + mxr[h, 2].astype(F32)
            ).astype(BF16)
        mz_cp = send_all(
            [(z_piece(mz, (z + d) % 8), mzr.at[d - 1], at_z(d)) for d in z_order], mzr
        )
        v_cp.wait_recv()
        for d in (1, 3, 2):
            gather_wait(b_cp, d)
        ig[...] = dot_tn(vcol[...], gball[...])
        ig_send[...] = ig[pl.ds(pl.multiple_of(own * (1 - k), 128), own), :].astype(BF16)
        ig_cp = send(ig_send, ig_recv, mate)
        ig_cp.wait_recv()
        ig_sum = (
            ig[pl.ds(pl.multiple_of(own * k, 128), own), :] + ig_recv[...].astype(F32)
        ).astype(BF16)
        for r in range(16):
            for s in range(2):
                ix[2 * r + s] = ig_sum[8 * r : 8 * (r + 1), half * s : half * (s + 1)]
        pl.semaphore_wait(ready, 3)
        ix_cp = send_all(
            [(ix.at[at_o(*f)[0]], ixr.at[n], at_o(*f)) for n, f in enumerate(others)], ixr
        )

        mz_cp.wait_recv()
        total = z_piece(mz, z)[...].astype(F32)
        for d in range(7):
            total += mzr[d].astype(F32)
        mf[...] = total.astype(BF16)
        mg_cp = send_all([(mf, z_piece(mg.at[x], z), at_z(d)) for d in z_order], mzr)
        mg[x, z // 2, :, pl.ds(pl.multiple_of(half * (z % 2), 128), half)] = mf[...]
        ix_cp.wait_recv()
        total = ix[obj].astype(F32)
        for n in range(len(others)):
            total += ixr[n].astype(F32)
        jf[...] = total.astype(BF16)
        jg_cp = send_all([(jf, jg.at[obj], at_o(*f)) for f in others], ixr)
        jg[obj] = jf[...]
        mg_cp.wait_recv()
        mo_cp = send_all([(mg.at[x], mg.at[x], at_x(d)) for d in (2, 1, 3)], mg.at[pl.ds(0, 3)])
        jg_cp.wait_recv()
        l_gin = load(9, jg, gin_hbm)
        mo_cp.wait_recv()
        l_main = load(0, mg, gmain_hbm)
        for cp in sent:
            cp.wait_send()
        l_latent.wait()
        l_gin.wait()
        l_main.wait()

    scratch = [
        ((views, patches), jnp.int32), ((width,), F32), ((own, width), BF16),
        ((CHUNKS, patches, cols), BF16), ((feat, width), BF16), ((width, 3 * width), BF16),
        ((width, width), BF16), ((own, width), BF16), ((2, group, patches), BF16),
        ((CHUNKS, group, cols), BF16), ((CHUNKS, group, cols), BF16), ((CHUNKS, group, cols), F32),
        ((CHUNKS, group, cols), BF16), ((CHUNKS, 2, own, cols // 2), BF16),
        ((CHUNKS, 2, own, cols), BF16),
        ((group, width), BF16), ((own, feat), BF16), ((group, vcols), BF16),
        ((own, width), F32), ((own, width), F32), ((group, width), BF16), ((width, group), BF16),
        ((width, 3 * part), BF16), ((group, part), BF16), ((slots, 2 * part), BF16),
        ((4, own, part), BF16), ((group, part), BF16), ((group, part), BF16), ((own, width), BF16),
        ((heads, group, 128), F32), ((heads, group, 128), BF16), ((heads, group, 128), BF16),
        ((heads, group, 256), BF16), ((heads, group, part), BF16), ((4, heads, own, 256), BF16),
        ((own, 3 * width), BF16),
        ((part, width), F32), ((orows, width), BF16), ((orows, width), BF16),
        ((heads, 8, orows, part), F32), ((heads, 4, orows, part), BF16),
        ((heads, 4, orows, part), BF16),
        ((4, orows, 2 * part), BF16), ((4, orows, part), BF16),
        ((4, orows, 2 * part), BF16), ((4, orows, part), BF16),
        ((group, width), BF16), ((2 * own, width), F32), ((own, width), BF16), ((own, width), BF16),
        ((4, 4, 24, width), BF16), ((4, 3, 24, width), BF16), ((4, 24, width), BF16),
        ((7, 24, width // 2), BF16), ((24, width // 2), BF16), ((4, 4, 24, width), BF16),
        ((objects, 8, width // 2), BF16), ((objects - 1, 8, width // 2), BF16),
        ((8, width // 2), BF16), ((objects, 8, width // 2), BF16),
    ]
    return kernel, scratch


def write_out(
    latent_hbm, gin_hbm, gmain_hbm, latent_out, in_out, qkv_out, out_out,
    latent_v, gin_v, gmain_v, in_v, qkv_v, out_v, lsem, osem,
):
    width = latent_v.shape[1]
    half = width // 2
    part = width // 4
    loads = [pltpu.make_async_copy(gmain_hbm.at[r], gmain_v.at[r], lsem.at[r]) for r in range(4)]
    loads.append(pltpu.make_async_copy(gin_hbm, gin_v, lsem.at[4]))
    loads.append(pltpu.make_async_copy(latent_hbm, latent_v, lsem.at[5]))
    for cp in loads:
        cp.start()
    stores = []

    def store(src, dst):
        cp = pltpu.make_async_copy(src, dst, osem.at[len(stores)])
        cp.start()
        stores.append(cp)

    for r in range(4):
        loads[r].wait()
        at = slice(24 * r, 24 * (r + 1))
        for s in range(3):
            for t in range(4):
                for h in range(3):
                    to = width * s + part * t + HEAD_DIM * h
                    fr = part * t + HEAD_DIM * s
                    qkv_v[at, to : to + HEAD_DIM] = gmain_v[r, h, :, fr : fr + HEAD_DIM].astype(F32)
        store(qkv_v.at[pl.ds(24 * r, 24)], qkv_out.at[pl.ds(24 * r, 24)])
        out_v[at, :] = gmain_v[r, 3].astype(F32)
    store(out_v, out_out)
    loads[4].wait()
    for r in range(16):
        for s in range(2):
            in_v[8 * r : 8 * (r + 1), half * s : half * (s + 1)] = gin_v[2 * r + s].astype(F32)
    store(in_v, in_out)
    loads[5].wait()
    store(latent_v, latent_out)
    for cp in stores:
        cp.wait()


def per_device(
    features, projection, active_count, in_weight, norm_gain, qkv_weight, out_weight, cotangent
):
    patches, feat = features.shape[2:]
    own, width = cotangent.shape[1:]
    views = projection.shape[1]
    objects = lax.axis_size("obj")
    kernel, scratch = make_kernel((patches, feat, width, own, objects, views))
    hbm = pl.BlockSpec(memory_space=pl.ANY)
    latent, gin, gmain = pl.pallas_call(
        kernel,
        name="encode",
        out_shape=(
            jax.ShapeDtypeStruct((own, width), BF16),
            jax.ShapeDtypeStruct((objects, 8, width // 2), BF16),
            jax.ShapeDtypeStruct((4, 4, 24, width), BF16),
        ),
        in_specs=[hbm] * 8,
        out_specs=(hbm, hbm, hbm),
        scratch_shapes=[pltpu.VMEM(s, t) for s, t in scratch]
        + [
            pltpu.SMEM((1,), jnp.int32),
            pltpu.SemaphoreType.DMA((56,)),
            pltpu.SemaphoreType.DMA((56,)),
            pltpu.SemaphoreType.DMA((10 + CHUNKS,)),
            pltpu.SemaphoreType.REGULAR,
        ],
        compiler_params=pltpu.CompilerParams(
            collective_id=0, has_side_effects=True, vmem_limit_bytes=62 * 1024 * 1024
        ),
    )(
        features.reshape(patches, feat),
        projection.reshape(views, patches),
        active_count,
        in_weight,
        norm_gain,
        qkv_weight,
        out_weight,
        cotangent.reshape(own, width),
    )
    latent, in_grad, qkv_grad, out_grad = pl.pallas_call(
        write_out,
        name="write_out",
        out_shape=(
            jax.ShapeDtypeStruct((own, width), BF16),
            jax.ShapeDtypeStruct((own, width), F32),
            jax.ShapeDtypeStruct((96, 3 * width), F32),
            jax.ShapeDtypeStruct((96, width), F32),
        ),
        in_specs=[hbm, hbm, hbm],
        out_specs=(hbm, hbm, hbm, hbm),
        scratch_shapes=[
            pltpu.VMEM((own, width), BF16),
            pltpu.VMEM((objects, 8, width // 2), BF16),
            pltpu.VMEM((4, 4, 24, width), BF16),
            pltpu.VMEM((own, width), F32),
            pltpu.VMEM((96, 3 * width), F32),
            pltpu.VMEM((96, width), F32),
            pltpu.SemaphoreType.DMA((6,)),
            pltpu.SemaphoreType.DMA((7,)),
        ],
    )(latent, gin, gmain)
    return (latent[None], in_grad, qkv_grad, out_grad)


def solution(mesh):
    return jax.shard_map(
        per_device,
        mesh=mesh,
        in_specs=(
            P("obj", "view", None, None),
            P("obj", None, None),
            P("obj"),
            P(),
            P(),
            P(),
            P(),
            P("obj", "view", None),
        ),
        out_specs=(P("obj", "view", None), P("view", None), P("view", None), P("view", None)),
        check_vma=False,
    )
```

time: 104 us -> 97.3 us (0.936)
  Pallas kernels: 103 us -> 95.7 us
    pallas_call x1, Pallas kernels: 100 us -> 93.3 us  [per_device(): pl.pallas_call(kernel, name='encode', out_shape=(jax.ShapeDtypeStruct((ow...]
where the time goes in v3:
time: 97.3 us; the launch traced here: 97.2 us
  Pallas kernels  95.7 us (98%)
  between operations  1.47 us (2%)
    pallas_call x1, Pallas kernels, per_device(): pl.pallas_call(kernel, name='encode', out_shape=(jax.ShapeDtypeStruct((ow...  93.3 us
    pallas_call x1, Pallas kernels, per_device(): pl.pallas_call(write_out, name='write_out', out_shape=(jax.ShapeDtypeStru...  2.39 us

profile of v3, /device:TPU:1, one launch (start us, length us, event | category | flops | bytes accessed | tf_op | source)
XLA Modules:
  0.0 97.2 jit_solution(16763222065761982298)
XLA Ops:
  1.3 93.3 %encode.1 = (bf16[128,768]{1,0:T(8,128)(2,1)}, bf16[32,8,384]{2,1,0:T(8,128)(2,1)}, bf16[4,4,24,768]{3,2,1,0:T(8,128)(2,1)}) custom-call(bf16[1369,1024]{1,0:T(8,128)(2,1)} %bitcast.4, s32[8,1369]{1,0:T(8,128)} %bitcast.6, s32[1]{0:T(128)S(6)} %copy.12.count_hbm, bf16[1024,768]{1,0:T(8,128)(2,1)} %in_hbm.1, f32[768]{0:T(1024)} %gain_hbm.1, ...), custom_call_target="tpu_custom_call" | custom-call | tf_op jit(solution)/shard_map/encode/pallas_call | solution.py:620
  94.6 2.4 %write_out.1 = (bf16[128,768]{1,0:T(8,128)(2,1)}, f32[128,768]{1,0:T(8,128)}, f32[96,2304]{1,0:T(8,128)}, f32[96,768]{1,0:T(8,128)}) custom-call(bf16[128,768]{1,0:T(8,128)(2,1)} %get-tuple-element.11.latent_hbm, bf16[32,8,384]{2,1,0:T(8,128)(2,1)} %get-tuple-element.12.gin_hbm, bf16[4,4,24,768]{3,2,1,0:T(8,128)(2,1)} %get-tuple-element.13.gmain_hbm), custom_call_target="tpu_custom_call" | custom-call | tf_op jit(solution)/shard_map/write_out/pallas_call | solution.py:651

commit v4 on v3

--- a/solution.py
+++ b/solution.py
@@ -51,11 +51,11 @@
     def kernel(
         feat_hbm, proj_hbm, count_hbm, in_hbm, gain_hbm, qkv_hbm, out_hbm, cot_hbm,
         latent_hbm, gin_hbm, gmain_hbm,
-        proj_ref, gain_ref, latent_v, feat_v, inw, qkvw, outw, cot_v, hot, psend, precv, pown, ysend, rrecv, yrecv,
-        seeds, vox, vcol, base, unit, normed, turned, wown, qs, kvs, gsend, gouts, att, afull,
-        dkv, dkv_send, dkv_recv, gp, gq, gpr, gpfull, og, og_send, og_recv,
-        qg, qg_send, qg_recv, qsum, qlast, qrecv, qrlast, gball, ig, ig_send, ig_recv,
-        mx, mxr, mz, mzr, mf, mg, ix, ixr, jf, jg,
+        proj_ref, gain_ref, latent_v, feat_v, inw, qkvw, outw, cot_v, hot, psend, precv, pown, ysend, psum, rrecv, yrecv, ylast,
+        seeds, vox, vcol, base, unit, normed, turned, wown, qs, kvs, gsend, gouts, wback, att, afull,
+        dkv, dkv_send, dkv_recv, gp, gq, gpr, og, og_send, og_recv,
+        qg, qg_send, qg_recv, qx, qxr, qxl, qxlr, qt, qr, ox, oxr, gball, ig, ig_send, ig_recv,
+        mz, mzr, mf, mg, ix, ixr, iz, izr, jf, jg,
         count_ref, ssem, rsem, lsem, ready,
     ):
         obj = lax.axis_index("obj")
@@ -169,52 +169,53 @@
                 )
                 hot[kk, own * d : own * (d + 1), :] = jnp.where(ids == proj_row, 1.0, 0.0).astype(BF16)
 
-        mate_cp, relay_cp, y_cp = [], [], []
+        mate_cp, relay_cp, y_cp = [], {}, {}
 
         def sums(j, kk):
             return dot_nn(hot[kk], feat_v[j])
 
+        last = CHUNKS - 1
+
         def combine(j):
+            raw = sums(j, 1)
             mate_cp[j].wait_recv()
-            both = pown[j] + precv[j].astype(F32)
-            pown[j] = both
-            far = slice(2 * own, 3 * own)
-            ysend[j, far, :] = both[far, :].astype(BF16)
-            relay_cp.append(
-                send_all(
-                    [
-                        (
-                            ysend.at[j, rows_of(2), pl.ds(cols // 2 * s, cols // 2)],
-                            rrecv.at[j, s],
-                            at_y((1, 3)[s]),
-                        )
-                        for s in range(2)
-                    ],
-                    rrecv.at[j],
+            both = raw + precv[j].astype(F32)
+            pown[j] = both[0:own, :]
+            ysend[j, own:, :] = both[own:, :].astype(BF16)
+            if j == last:
+                y_cp[j] = send_all(
+                    [(ysend.at[j, rows_of(d)], ylast.at[d - 1], at_y(4 - d)) for d in (2, 3, 1)],
+                    ylast,
                 )
+                return
+            relay_cp[j] = send_all(
+                [
+                    (
+                        ysend.at[j, rows_of(2), pl.ds(cols // 2 * s, cols // 2)],
+                        rrecv.at[j, s],
+                        at_y((1, 3)[s]),
+                    )
+                    for s in range(2)
+                ],
+                rrecv.at[j],
             )
+            mid = cols // 2
+            psum[j, 0] = both[3 * own :, 0:mid]
+            psum[j, 1] = both[own : 2 * own, mid:]
 
         def forward(j):
             relay_cp[j].wait_recv()
             mid = cols // 2
             for s, d in ((0, 3), (1, 1)):
-                at = slice(own * d, own * (d + 1))
-                block = pown[j, at, :]
-                passed = rrecv[j, s].astype(F32)
-                if s == 0:
-                    ysend[j, at, 0:mid] = (block[:, 0:mid] + passed).astype(BF16)
-                    ysend[j, at, mid:] = block[:, mid:].astype(BF16)
-                else:
-                    ysend[j, at, 0:mid] = block[:, 0:mid].astype(BF16)
-                    ysend[j, at, mid:] = (block[:, mid:] + passed).astype(BF16)
-            y_cp.append(
-                send_all(
-                    [
-                        (ysend.at[j, rows_of(d)], yrecv.at[j, s], at_y(4 - d))
-                        for s, d in ((0, 3), (1, 1))
-                    ],
-                    yrecv.at[j],
-                )
+                ysend[j, own * d : own * (d + 1), mid * s : mid * (s + 1)] = (
+                    psum[j, s] + rrecv[j, s].astype(F32)
+                ).astype(BF16)
+            y_cp[j] = send_all(
+                [
+                    (ysend.at[j, rows_of(d)], yrecv.at[j, s], at_y(4 - d))
+                    for s, d in ((0, 3), (1, 1))
+                ],
+                yrecv.at[j],
             )
 
         l_cot.wait()
@@ -225,6 +226,45 @@
         mate_cp.append(send(psend.at[0], precv.at[0], mate))
         for p in range(1, 4):
             pl.semaphore_signal(ready, 1, device_id=at_x(p), device_id_type=MESH)
+        for j in range(1, CHUNKS):
+            l_feat[j].wait()
+            psend[j] = sums(j, 0).astype(BF16)
+            mate_cp.append(send(psend.at[j], precv.at[j], mate))
+            combine(j - 1)
+            if j > 1:
+                forward(j - 2)
+        combine(last)
+        forward(last - 1)
+
+        number = jnp.zeros((own, 1), F32)
+        for w in range(views):
+            same = proj_ref[w : w + 1, :] == view * own + lax.broadcasted_iota(
+                jnp.int32, (own, patches), 0
+            )
+            number += jnp.sum(jnp.where(same, 1.0, 0.0), axis=1, keepdims=True)
+        number = jnp.maximum(number, 1.0)
+
+        l_qkv.wait()
+        for t in range(3):
+            window = qkvw[:, pl.ds(pl.multiple_of(width * t + 128 * ((3 * c) // 2), 128), 256)]
+
+            @pl.when(c % 2 == 0)
+            def _():
+                wown[:, part * t : part * (t + 1)] = window[:, 0:part]
+
+            @pl.when(c % 2 == 1)
+            def _():
+                wown[:, part * t : part * (t + 1)] = window[:, 64 : 64 + part]
+
+        for t in range(4):
+            for h in range(heads):
+                at = part * t + HEAD_DIM * h
+                w_q = qkvw[:, at : at + HEAD_DIM]
+                wback[t, h, :, 0:128] = jnp.concatenate([w_q, jnp.zeros_like(w_q)], axis=1)
+                wback[t, h, :, 128:] = jnp.concatenate(
+                    [qkvw[:, s * width + at : s * width + at + HEAD_DIM] for s in (1, 2)], axis=1
+                )
+
         l_out.wait()
         for t in range(4):
             gsend[t] = dot_nt(seeds[0:own, :], outw[part * t : part * (t + 1), :]).astype(BF16)
@@ -233,43 +273,14 @@
             gouts.at[pl.ds(0, 3 * own)],
         )
         gouts[0:own, :] = gsend[c]
-        pown[0] = sums(0, 1)
-        for j in range(1, CHUNKS):
-            l_feat[j].wait()
-            psend[j] = sums(j, 0).astype(BF16)
-            mate_cp.append(send(psend.at[j], precv.at[j], mate))
-            combine(j - 1)
-            pown[j] = sums(j, 1)
-            if j > 1:
-                forward(j - 2)
-        combine(CHUNKS - 1)
-        forward(CHUNKS - 2)
-
-        number = jnp.zeros((own, 1), F32)
-        for w in range(views):
-            same = proj_ref[w : w + 1, :] == view * own + lax.broadcasted_iota(
-                jnp.int32, (own, patches), 0
-            )
-            number += jnp.sum(jnp.where(same, 1.0, 0.0), axis=1, keepdims=True)
-        number = jnp.maximum(number, 1.0)
-        forward(CHUNKS - 1)
-
-        l_qkv.wait()
-        for t in range(3):
-            window = qkvw[:, pl.ds(pl.multiple_of(width * t + 128 * ((3 * c) // 2), 128), 256)]
-
-            @pl.when(c % 2 == 0)
-            def _():
-                wown[:, part * t : part * (t + 1)] = window[:, 0:part]
-
-            @pl.when(c % 2 == 1)
-            def _():
-                wown[:, part * t : part * (t + 1)] = window[:, 64 : 64 + part]
-
         for j in range(CHUNKS):
-            total = pown[j, 0:own, :]
+            total = pown[j]
             y_cp[j].wait_recv()
-            total += yrecv[j, 0].astype(F32) + yrecv[j, 1].astype(F32)
+            if j == last:
+                for d in range(3):
+                    total += ylast[d].astype(F32)
+            else:
+                total += yrecv[j, 0].astype(F32) + yrecv[j, 1].astype(F32)
             vox[:, cols * j : cols * (j + 1)] = (total / number).astype(BF16)
         l_in.wait()
         base_rows = dot_nn(vox[...], inw[...])
@@ -324,7 +335,7 @@
         kv_cp.wait_recv()
         o_cp.wait_recv()
 
-        dkv_cp, g_cp, qg_cp, t_cp = [], [], [], []
+        dkv_cp, g_cp, qg_cp, x_cp = [], [], [], []
 
         def attend(h):
             hs = slice(HEAD_DIM * h, HEAD_DIM * (h + 1))
@@ -378,48 +389,54 @@
             qg_cp[h].wait_recv()
             for t in range(4):
                 block = (qg[h, 2 * t + k] + qg_recv[h, t].astype(F32)).astype(BF16)
-                if h < 2:
-                    qsum[t, :, part * h : part * (h + 1)] = block
-                else:
-                    qlast[t] = block
+                for r in range(4):
+                    piece = block[24 * r : 24 * (r + 1), :]
+                    if h < 2:
+                        qx[r, t, :, part * h : part * (h + 1)] = piece
+                    else:
+                        qxl[r, t] = piece
             if h:
-                buf, recv = (qsum, qrecv) if h == 1 else (qlast, qrlast)
-                t_cp.append(
+                buf, recv = (qx, qxr) if h == 1 else (qxl, qxlr)
+                x_cp.append(
                     send_all(
-                        [(buf.at[(c + d) % 4], recv.at[c], at_y(d)) for d in (2, 1, 3)],
-                        recv.at[pl.ds(0, 3)],
+                        [(buf.at[(x + d) % 4], recv.at[d - 1], at_x(d)) for d in (2, 1, 3)], recv
                     )
                 )
-                recv[c] = buf[c]
-
-        def x_scatter(h):
-            return send_all(
-                [(mx.at[h, (x + d) % 4], mxr.at[h, d - 1], at_x(d)) for d in (2, 1, 3)],
-                mxr.at[h],
+
+        def turn():
+            for n, (buf, recv) in enumerate(((qx, qxr), (qxl, qxlr))):
+                x_cp[n].wait_recv()
+                for t in range(4):
+                    at = slice(2 * part * n, 2 * part + part * n)
+                    qt[t, :, at] = (
+                        buf[x, t].astype(F32)
+                        + recv[0, t].astype(F32)
+                        + recv[1, t].astype(F32)
+                        + recv[2, t].astype(F32)
+                    ).astype(BF16)
+            cp = send_all(
+                [(qt.at[(c + d) % 4], qr.at[c], at_y(d)) for d in (2, 1, 3)], qr.at[pl.ds(0, 3)]
             )
-
-        def join(h):
+            qr[c] = qt[c]
+            return cp
+
+        def back(h):
+            g_cp[h].wait_recv()
+            total = jnp.zeros((own, width), F32)
             for t in range(4):
-                for r in range(4):
-                    rows = slice(24 * r, 24 * (r + 1))
-                    if h < 2:
-                        block = qrecv[t, rows, part * h : part * (h + 1)]
-                    else:
-                        block = qrlast[t, rows, :]
-                    mx[h, r, :, part * t : part * (t + 1)] = block
-            mx_cp.append(x_scatter(h))
-
-        def place(h):
-            g_cp[h].wait_recv()
-            for t in range(4):
-                for s3, lo in ((0, 0), (1, 128), (2, 192)):
-                    at = width * s3 + part * t + HEAD_DIM * h
-                    gpfull[:, at : at + HEAD_DIM] = gpr[t, h, :, lo : lo + HEAD_DIM]
                 at = part * t + HEAD_DIM * h
                 afull[:, at : at + HEAD_DIM] = gpr[t, h, :, HEAD_DIM : 2 * HEAD_DIM]
+                total += dot_nt(gpr[t, h], wback[t, h])
+            return total
 
         attend(0)
+        attend(1)
         gather_pass(seeds, s_cp)
+        finish(0)
+        attend(2)
+        finish(1)
+        swap(0)
+        finish(2)
         v_cp = send_all(
             [
                 (
@@ -432,30 +449,10 @@
             vcol.at[pl.ds(0, 3 * own)],
         )
         vcol[0:own, :] = vox[:, pl.ds(pl.multiple_of(vcols * c, 128), vcols)]
-        attend(1)
-        finish(0)
-        attend(2)
-        finish(1)
-        swap(0)
-        for d in (1, 3, 2):
-            gather_wait(s_cp, d)
-        og[...] = dot_tn(att[...], seeds[...])
-        og_send[...] = og[pl.ds(pl.multiple_of(orows * (1 - k), 32), orows), :].astype(BF16)
-        og_cp = send(og_send, og_recv, mate)
-        finish(2)
         swap(1)
         swap(2)
-        place(0)
-        place(1)
-        og_cp.wait_recv()
-        og_sum = (
-            og[pl.ds(pl.multiple_of(orows * k, 32), orows), :] + og_recv[...].astype(F32)
-        ).astype(BF16)
-        for r in range(4):
-            mx[3, r] = og_sum[24 * r : 24 * (r + 1), :]
-        mx_cp = [x_scatter(3)]
-        place(2)
-        grad_unit = dot_nt(gpfull[...], qkvw[...]) * gain
+        early = back(0) + back(1)
+        grad_unit = (early + back(2)) * gain
         unit_rows = unit[...]
         branch_grad = inverse * (
             grad_unit
@@ -465,11 +462,12 @@
         gball[0:own, :] = (seeds[0:own, :].astype(F32) + branch_grad).astype(BF16)
         b_cp = gather_start(gball)
 
-        t_cp[0].wait_recv()
-        join(0)
-        join(1)
-        t_cp[1].wait_recv()
-        join(2)
+        for d in (1, 3, 2):
+            gather_wait(s_cp, d)
+        og[...] = dot_tn(att[...], seeds[...])
+        og_send[...] = og[pl.ds(pl.multiple_of(orows * (1 - k), 32), orows), :].astype(BF16)
+        og_cp = send(og_send, og_recv, mate)
+        t_cp = turn()
 
         half = width // 2
         z_order = (4, 3, 5, 2, 6, 1, 7)
@@ -478,19 +476,25 @@
             return buf.at[where // 2, :, pl.ds(pl.multiple_of(half * (where % 2), 128), half)]
 
         gather_pass(gball, b_cp)
+        og_cp.wait_recv()
+        og_sum = (
+            og[pl.ds(pl.multiple_of(orows * k, 32), orows), :] + og_recv[...].astype(F32)
+        ).astype(BF16)
+        for r in range(4):
+            ox[r] = og_sum[24 * r : 24 * (r + 1), :]
+        ox_cp = send_all([(ox.at[(x + d) % 4], oxr.at[d - 1], at_x(d)) for d in (2, 1, 3)], oxr)
         branch = dot_nn(afull[...], outw[...])
         latent_v[...] = (live * (base[...] + branch)).astype(BF16)
         l_latent = load(8, latent_v, latent_hbm)
 
-        for cp in mx_cp:
-            cp.wait_recv()
-        for h in range(4):
-            mz[h] = (
-                mx[h, x].astype(F32)
-                + mxr[h, 0].astype(F32)
-                + mxr[h, 1].astype(F32)
-                + mxr[h, 2].astype(F32)
-            ).astype(BF16)
+        ox_cp.wait_recv()
+        mz[3] = (
+            ox[x].astype(F32) + oxr[0].astype(F32) + oxr[1].astype(F32) + oxr[2].astype(F32)
+        ).astype(BF16)
+        t_cp.wait_recv()
+        for h in range(heads):
+            for t in range(4):
+                mz[h, :, part * t : part * (t + 1)] = qr[t, :, part * h : part * (h + 1)]
         mz_cp = send_all(
             [(z_piece(mz, (z + d) % 8), mzr.at[d - 1], at_z(d)) for d in z_order], mzr
         )
@@ -506,28 +510,58 @@
         ).astype(BF16)
         for r in range(16):
             for s in range(2):
-                ix[2 * r + s] = ig_sum[8 * r : 8 * (r + 1), half * s : half * (s + 1)]
-        pl.semaphore_wait(ready, 3)
-        ix_cp = send_all(
-            [(ix.at[at_o(*f)[0]], ixr.at[n], at_o(*f)) for n, f in enumerate(others)], ixr
-        )
+                p = 2 * r + s
+                ix[p // 8, p % 8] = ig_sum[8 * r : 8 * (r + 1), half * s : half * (s + 1)]
+        ix_cp = send_all([(ix.at[(x + d) % 4], ixr.at[d - 1], at_x(d)) for d in (2, 1, 3)], ixr)
 
         mz_cp.wait_recv()
         total = z_piece(mz, z)[...].astype(F32)
         for d in range(7):
             total += mzr[d].astype(F32)
         mf[...] = total.astype(BF16)
-        mg_cp = send_all([(mf, z_piece(mg.at[x], z), at_z(d)) for d in z_order], mzr)
+        near, far = (1, 7, 2, 6), (3, 4, 5)
+        mg_cp = [
+            send_all([(mf, z_piece(mg.at[x], z), at_z(d)) for d in ds], mzr.at[pl.ds(0, len(ds))])
+            for ds in (near, far)
+        ]
         mg[x, z // 2, :, pl.ds(pl.multiple_of(half * (z % 2), 128), half)] = mf[...]
+        mo_n = used[0]
+        used[0] += 1
+
+        def spread(src, where):
+            for d in (2, 1, 3):
+                pltpu.make_async_remote_copy(
+                    src_ref=src, dst_ref=z_piece(mg.at[x], where),
+                    send_sem=ssem.at[mo_n], recv_sem=rsem.at[mo_n],
+                    device_id=at_x(d), device_id_type=MESH,
+                ).start()
+
+        mo_cp = Group(mg.at[pl.ds(0, 3)], ssem.at[mo_n], rsem.at[mo_n])
+        sent.append(mo_cp)
+        spread(mf, z)
         ix_cp.wait_recv()
-        total = ix[obj].astype(F32)
-        for n in range(len(others)):
-            total += ixr[n].astype(F32)
+        for p in range(8):
+            iz[p] = (
+                ix[x, p].astype(F32)
+                + ixr[0, p].astype(F32)
+                + ixr[1, p].astype(F32)
+                + ixr[2, p].astype(F32)
+            ).astype(BF16)
+        iz_cp = send_all([(iz.at[(z + d) % 8], izr.at[d - 1], at_z(d)) for d in z_order], izr)
+        for cp, ds in zip(mg_cp, (near, far)):
+            cp.wait_recv()
+            for d in ds:
+                spread(z_piece(mg.at[x], (z + 8 - d) % 8), (z + 8 - d) % 8)
+        iz_cp.wait_recv()
+        total = iz[z].astype(F32)
+        for d in range(7):
+            total += izr[d].astype(F32)
         jf[...] = total.astype(BF16)
-        jg_cp = send_all([(jf, jg.at[obj], at_o(*f)) for f in others], ixr)
-        jg[obj] = jf[...]
-        mg_cp.wait_recv()
-        mo_cp = send_all([(mg.at[x], mg.at[x], at_x(d)) for d in (2, 1, 3)], mg.at[pl.ds(0, 3)])
+        pl.semaphore_wait(ready, 3)
+        jg_cp = send_all(
+            [(jf, jg.at[x * 8 + z], at_o(*f)) for f in others], jg.at[pl.ds(0, len(others))]
+        )
+        jg[x * 8 + z] = jf[...]
         jg_cp.wait_recv()
         l_gin = load(9, jg, gin_hbm)
         mo_cp.wait_recv()
@@ -542,25 +576,29 @@
         ((views, patches), jnp.int32), ((width,), F32), ((own, width), BF16),
         ((CHUNKS, patches, cols), BF16), ((feat, width), BF16), ((width, 3 * width), BF16),
         ((width, width), BF16), ((own, width), BF16), ((2, group, patches), BF16),
-        ((CHUNKS, group, cols), BF16), ((CHUNKS, group, cols), BF16), ((CHUNKS, group, cols), F32),
-        ((CHUNKS, group, cols), BF16), ((CHUNKS, 2, own, cols // 2), BF16),
-        ((CHUNKS, 2, own, cols), BF16),
+        ((CHUNKS, group, cols), BF16), ((CHUNKS, group, cols), BF16), ((CHUNKS, own, cols), F32),
+        ((CHUNKS, group, cols), BF16), ((CHUNKS - 1, 2, own, cols // 2), F32),
+        ((CHUNKS - 1, 2, own, cols // 2), BF16), ((CHUNKS - 1, 2, own, cols), BF16),
+        ((3, own, cols), BF16),
         ((group, width), BF16), ((own, feat), BF16), ((group, vcols), BF16),
         ((own, width), F32), ((own, width), F32), ((group, width), BF16), ((width, group), BF16),
         ((width, 3 * part), BF16), ((group, part), BF16), ((slots, 2 * part), BF16),
-        ((4, own, part), BF16), ((group, part), BF16), ((group, part), BF16), ((own, width), BF16),
+        ((4, own, part), BF16), ((group, part), BF16), ((4, heads, width, 256), BF16),
+        ((group, part), BF16), ((own, width), BF16),
         ((heads, group, 128), F32), ((heads, group, 128), BF16), ((heads, group, 128), BF16),
         ((heads, group, 256), BF16), ((heads, group, part), BF16), ((4, heads, own, 256), BF16),
-        ((own, 3 * width), BF16),
         ((part, width), F32), ((orows, width), BF16), ((orows, width), BF16),
         ((heads, 8, orows, part), F32), ((heads, 4, orows, part), BF16),
         ((heads, 4, orows, part), BF16),
-        ((4, orows, 2 * part), BF16), ((4, orows, part), BF16),
-        ((4, orows, 2 * part), BF16), ((4, orows, part), BF16),
+        ((4, 4, 24, 2 * part), BF16), ((3, 4, 24, 2 * part), BF16),
+        ((4, 4, 24, part), BF16), ((3, 4, 24, part), BF16),
+        ((4, 24, 3 * part), BF16), ((4, 24, 3 * part), BF16),
+        ((4, 24, width), BF16), ((3, 24, width), BF16),
         ((group, width), BF16), ((2 * own, width), F32), ((own, width), BF16), ((own, width), BF16),
-        ((4, 4, 24, width), BF16), ((4, 3, 24, width), BF16), ((4, 24, width), BF16),
+        ((4, 24, width), BF16),
         ((7, 24, width // 2), BF16), ((24, width // 2), BF16), ((4, 4, 24, width), BF16),
-        ((objects, 8, width // 2), BF16), ((objects - 1, 8, width // 2), BF16),
+        ((4, 8, 8, width // 2), BF16), ((3, 8, 8, width // 2), BF16),
+        ((8, 8, width // 2), BF16), ((7, 8, width // 2), BF16),
         ((8, width // 2), BF16), ((objects, 8, width // 2), BF16),
     ]
     return kernel, scratch

time: 97.3 us -> 94.6 us (0.972)
  the two profiles are of different devices: /device:TPU:1 before, /device:TPU:9 now
where the time goes in v4:
time: 94.6 us; the launch traced here: 94.5 us
  Pallas kernels  93 us (98%)
  between operations  1.47 us (2%)
    pallas_call x1, Pallas kernels, per_device(): pl.pallas_call(kernel, name='encode', out_shape=(jax.ShapeDtypeStruct((ow...  90.6 us
    pallas_call x1, Pallas kernels, per_device(): pl.pallas_call(write_out, name='write_out', out_shape=(jax.ShapeDtypeStru...  2.39 us

profile of v4, /device:TPU:9, one launch (start us, length us, event | category | flops | bytes accessed | tf_op | source)
XLA Modules:
  0.0 94.5 jit_solution(12077176059630543584)
XLA Ops:
  1.3 90.6 %encode.1 = (bf16[128,768]{1,0:T(8,128)(2,1)}, bf16[32,8,384]{2,1,0:T(8,128)(2,1)}, bf16[4,4,24,768]{3,2,1,0:T(8,128)(2,1)}) custom-call(bf16[1369,1024]{1,0:T(8,128)(2,1)} %bitcast.4, s32[8,1369]{1,0:T(8,128)} %bitcast.6, s32[1]{0:T(128)S(6)} %copy.12.count_hbm, bf16[1024,768]{1,0:T(8,128)(2,1)} %in_hbm.1, f32[768]{0:T(1024)} %gain_hbm.1, ...), custom_call_target="tpu_custom_call" | custom-call | tf_op jit(solution)/shard_map/encode/pallas_call | solution.py:658
  91.9 2.4 %write_out.1 = (bf16[128,768]{1,0:T(8,128)(2,1)}, f32[128,768]{1,0:T(8,128)}, f32[96,2304]{1,0:T(8,128)}, f32[96,768]{1,0:T(8,128)}) custom-call(bf16[128,768]{1,0:T(8,128)(2,1)} %get-tuple-element.11.latent_hbm, bf16[32,8,384]{2,1,0:T(8,128)(2,1)} %get-tuple-element.12.gin_hbm, bf16[4,4,24,768]{3,2,1,0:T(8,128)(2,1)} %get-tuple-element.13.gmain_hbm), custom_call_target="tpu_custom_call" | custom-call | tf_op jit(solution)/shard_map/write_out/pallas_call | solution.py:689

commit v5 on v4

--- a/solution.py
+++ b/solution.py
@@ -52,7 +52,7 @@
         feat_hbm, proj_hbm, count_hbm, in_hbm, gain_hbm, qkv_hbm, out_hbm, cot_hbm,
         latent_hbm, gin_hbm, gmain_hbm,
         proj_ref, gain_ref, latent_v, feat_v, inw, qkvw, outw, cot_v, hot, psend, precv, pown, ysend, psum, rrecv, yrecv, ylast,
-        seeds, vox, vcol, base, unit, normed, turned, wown, qs, kvs, gsend, gouts, wback, att, afull,
+        seeds, vox, vcol, base, unit, normed, turned, wown, qs, kvs, gouts, wback, att, afull,
         dkv, dkv_send, dkv_recv, gp, gq, gpr, og, og_send, og_recv,
         qg, qg_send, qg_recv, qx, qxr, qxl, qxlr, qt, qr, ox, oxr, gball, ig, ig_send, ig_recv,
         mz, mzr, mf, mg, ix, ixr, iz, izr, jf, jg,
@@ -226,11 +226,14 @@
         mate_cp.append(send(psend.at[0], precv.at[0], mate))
         for p in range(1, 4):
             pl.semaphore_signal(ready, 1, device_id=at_x(p), device_id_type=MESH)
+        s_cp = gather_start(seeds)
         for j in range(1, CHUNKS):
             l_feat[j].wait()
             psend[j] = sums(j, 0).astype(BF16)
             mate_cp.append(send(psend.at[j], precv.at[j], mate))
             combine(j - 1)
+            if j == 2:
+                gather_pass(seeds, s_cp)
             if j > 1:
                 forward(j - 2)
         combine(last)
@@ -266,13 +269,16 @@
                 )
 
         l_out.wait()
-        for t in range(4):
-            gsend[t] = dot_nt(seeds[0:own, :], outw[part * t : part * (t + 1), :]).astype(BF16)
-        o_cp = send_all(
-            [(gsend.at[(c + d) % 4], gouts.at[rows_of(d)], at_y(d)) for d in (2, 1, 3)],
-            gouts.at[pl.ds(0, 3 * own)],
-        )
-        gouts[0:own, :] = gsend[c]
+        rows = outw[pl.ds(pl.multiple_of(part * c, 64), part), :]
+
+        def pull(d):
+            at = slice(own * d, own * (d + 1))
+            if d:
+                gather_wait(s_cp, d)
+            gouts[at, :] = dot_nt(seeds[at, :], rows).astype(BF16)
+
+        for d in (0, 1, 3):
+            pull(d)
         for j in range(CHUNKS):
             total = pown[j]
             y_cp[j].wait_recv()
@@ -318,12 +324,24 @@
 
         project(0)
         gather_pass(normed, n_cp)
+        pull(2)
         for d in (1, 3):
             gather_wait(n_cp, d)
             project(d)
         gather_wait(n_cp, 2)
         project(2)
-        s_cp = gather_start(seeds)
+        v_cp = send_all(
+            [
+                (
+                    vox.at[:, pl.ds(pl.multiple_of(vcols * ((c + d) % 4), 128), vcols)],
+                    vcol.at[rows_of(d)],
+                    at_y(d),
+                )
+                for d in (1, 2, 3)
+            ],
+            vcol.at[pl.ds(0, 3 * own)],
+        )
+        vcol[0:own, :] = vox[:, pl.ds(pl.multiple_of(vcols * c, 128), vcols)]
 
         lane = lax.broadcasted_iota(jnp.int32, (1, own), 1)
         pieces = []
@@ -333,7 +351,6 @@
                 pieces.append(jnp.where(ids < count, 0.0, NEG).astype(F32))
         bias = jnp.concatenate(pieces, axis=1)
         kv_cp.wait_recv()
-        o_cp.wait_recv()
 
         dkv_cp, g_cp, qg_cp, x_cp = [], [], [], []
 
@@ -431,26 +448,23 @@
 
         attend(0)
         attend(1)
-        gather_pass(seeds, s_cp)
         finish(0)
         attend(2)
         finish(1)
         swap(0)
+        og[...] = dot_tn(att[...], seeds[...])
+        og_send[...] = og[pl.ds(pl.multiple_of(orows * (1 - k), 32), orows), :].astype(BF16)
+        og_cp = send(og_send, og_recv, mate)
         finish(2)
-        v_cp = send_all(
-            [
-                (
-                    vox.at[:, pl.ds(pl.multiple_of(vcols * ((c + d) % 4), 128), vcols)],
-                    vcol.at[rows_of(d)],
-                    at_y(d),
-                )
-                for d in (1, 2, 3)
-            ],
-            vcol.at[pl.ds(0, 3 * own)],
-        )
-        vcol[0:own, :] = vox[:, pl.ds(pl.multiple_of(vcols * c, 128), vcols)]
         swap(1)
         swap(2)
+        og_cp.wait_recv()
+        og_sum = (
+            og[pl.ds(pl.multiple_of(orows * k, 32), orows), :] + og_recv[...].astype(F32)
+        ).astype(BF16)
+        for r in range(4):
+            ox[r] = og_sum[24 * r : 24 * (r + 1), :]
+        ox_cp = send_all([(ox.at[(x + d) % 4], oxr.at[d - 1], at_x(d)) for d in (2, 1, 3)], oxr)
         early = back(0) + back(1)
         grad_unit = (early + back(2)) * gain
         unit_rows = unit[...]
@@ -462,11 +476,6 @@
         gball[0:own, :] = (seeds[0:own, :].astype(F32) + branch_grad).astype(BF16)
         b_cp = gather_start(gball)
 
-        for d in (1, 3, 2):
-            gather_wait(s_cp, d)
-        og[...] = dot_tn(att[...], seeds[...])
-        og_send[...] = og[pl.ds(pl.multiple_of(orows * (1 - k), 32), orows), :].astype(BF16)
-        og_cp = send(og_send, og_recv, mate)
         t_cp = turn()
 
         half = width // 2
@@ -476,13 +485,6 @@
             return buf.at[where // 2, :, pl.ds(pl.multiple_of(half * (where % 2), 128), half)]
 
         gather_pass(gball, b_cp)
-        og_cp.wait_recv()
-        og_sum = (
-            og[pl.ds(pl.multiple_of(orows * k, 32), orows), :] + og_recv[...].astype(F32)
-        ).astype(BF16)
-        for r in range(4):
-            ox[r] = og_sum[24 * r : 24 * (r + 1), :]
-        ox_cp = send_all([(ox.at[(x + d) % 4], oxr.at[d - 1], at_x(d)) for d in (2, 1, 3)], oxr)
         branch = dot_nn(afull[...], outw[...])
         latent_v[...] = (live * (base[...] + branch)).astype(BF16)
         l_latent = load(8, latent_v, latent_hbm)
@@ -583,7 +585,7 @@
         ((group, width), BF16), ((own, feat), BF16), ((group, vcols), BF16),
         ((own, width), F32), ((own, width), F32), ((group, width), BF16), ((width, group), BF16),
         ((width, 3 * part), BF16), ((group, part), BF16), ((slots, 2 * part), BF16),
-        ((4, own, part), BF16), ((group, part), BF16), ((4, heads, width, 256), BF16),
+        ((group, part), BF16), ((4, heads, width, 256), BF16),
         ((group, part), BF16), ((own, width), BF16),
         ((heads, group, 128), F32), ((heads, group, 128), BF16), ((heads, group, 128), BF16),
         ((heads, group, 256), BF16), ((heads, group, part), BF16), ((4, heads, own, 256), BF16),

time: 94.6 us -> 91.5 us (0.967)
  the two profiles are of different devices: /device:TPU:9 before, /device:TPU:1 now
where the time goes in v5:
time: 91.5 us; the launch traced here: 91.4 us
  Pallas kernels  90 us (98%)
  between operations  1.47 us (2%)
    pallas_call x1, Pallas kernels, per_device(): pl.pallas_call(kernel, name='encode', out_shape=(jax.ShapeDtypeStruct((ow...  87.6 us
    pallas_call x1, Pallas kernels, per_device(): pl.pallas_call(write_out, name='write_out', out_shape=(jax.ShapeDtypeStru...  2.39 us

profile of v5, /device:TPU:1, one launch (start us, length us, event | category | flops | bytes accessed | tf_op | source)
XLA Modules:
  0.0 91.4 jit_solution(16003435584627170317)
XLA Ops:
  1.3 87.6 %encode.1 = (bf16[128,768]{1,0:T(8,128)(2,1)}, bf16[32,8,384]{2,1,0:T(8,128)(2,1)}, bf16[4,4,24,768]{3,2,1,0:T(8,128)(2,1)}) custom-call(bf16[1369,1024]{1,0:T(8,128)(2,1)} %bitcast.4, s32[8,1369]{1,0:T(8,128)} %bitcast.6, s32[1]{0:T(128)S(6)} %copy.12.count_hbm, bf16[1024,768]{1,0:T(8,128)(2,1)} %in_hbm.1, f32[768]{0:T(1024)} %gain_hbm.1, ...), custom_call_target="tpu_custom_call" | custom-call | tf_op jit(solution)/shard_map/encode/pallas_call | solution.py:660
  88.9 2.4 %write_out.1 = (bf16[128,768]{1,0:T(8,128)(2,1)}, f32[128,768]{1,0:T(8,128)}, f32[96,2304]{1,0:T(8,128)}, f32[96,768]{1,0:T(8,128)}) custom-call(bf16[128,768]{1,0:T(8,128)(2,1)} %get-tuple-element.11.latent_hbm, bf16[32,8,384]{2,1,0:T(8,128)(2,1)} %get-tuple-element.12.gin_hbm, bf16[4,4,24,768]{3,2,1,0:T(8,128)(2,1)} %get-tuple-element.13.gmain_hbm), custom_call_target="tpu_custom_call" | custom-call | tf_op jit(solution)/shard_map/write_out/pallas_call | solution.py:691

commit v6 on v5

--- a/solution.py
+++ b/solution.py
@@ -354,7 +354,7 @@
 
         dkv_cp, g_cp, qg_cp, x_cp = [], [], [], []
 
-        def attend(h):
+        def attend(h, between=None):
             hs = slice(HEAD_DIM * h, HEAD_DIM * (h + 1))
             keys = kvs[:, hs]
             values = kvs[:, part + HEAD_DIM * h : part + HEAD_DIM * (h + 1)]
@@ -377,6 +377,8 @@
                 gp[h, rs, 0:128] = jnp.concatenate([grad_q, mixed.astype(BF16)], axis=1)
                 grad_k += dot_tn(gs, q)
                 grad_v += dot_tn(p, go)
+                if b == 0 and between is not None:
+                    between()
             both = jnp.concatenate([grad_k, grad_v], axis=1)
             dkv_send[h] = both[group:].astype(BF16)
             dkv_cp.append(send(dkv_send.at[h], dkv_recv.at[h], mate))
@@ -447,10 +449,8 @@
             return total
 
         attend(0)
-        attend(1)
-        finish(0)
-        attend(2)
-        finish(1)
+        attend(1, lambda: finish(0))
+        attend(2, lambda: finish(1))
         swap(0)
         og[...] = dot_tn(att[...], seeds[...])
         og_send[...] = og[pl.ds(pl.multiple_of(orows * (1 - k), 32), orows), :].astype(BF16)

time: 91.5 us -> 91.5 us (level)
  no operation moved by 1% of the time
where the time goes in v6:
time: 91.5 us; the launch traced here: 91.3 us
  Pallas kernels  89.9 us (98%)
  between operations  1.47 us (2%)
    pallas_call x1, Pallas kernels, per_device(): pl.pallas_call(kernel, name='encode', out_shape=(jax.ShapeDtypeStruct((ow...  87.5 us
    pallas_call x1, Pallas kernels, per_device(): pl.pallas_call(write_out, name='write_out', out_shape=(jax.ShapeDtypeStru...  2.39 us

profile of v6, /device:TPU:1, one launch (start us, length us, event | category | flops | bytes accessed | tf_op | source)
XLA Modules:
  0.0 91.3 jit_solution(3396896279097179200)
XLA Ops:
  1.3 87.5 %encode.1 = (bf16[128,768]{1,0:T(8,128)(2,1)}, bf16[32,8,384]{2,1,0:T(8,128)(2,1)}, bf16[4,4,24,768]{3,2,1,0:T(8,128)(2,1)}) custom-call(bf16[1369,1024]{1,0:T(8,128)(2,1)} %bitcast.4, s32[8,1369]{1,0:T(8,128)} %bitcast.6, s32[1]{0:T(128)S(6)} %copy.12.count_hbm, bf16[1024,768]{1,0:T(8,128)(2,1)} %in_hbm.1, f32[768]{0:T(1024)} %gain_hbm.1, ...), custom_call_target="tpu_custom_call" | custom-call | tf_op jit(solution)/shard_map/encode/pallas_call | solution.py:660
  88.8 2.4 %write_out.1 = (bf16[128,768]{1,0:T(8,128)(2,1)}, f32[128,768]{1,0:T(8,128)}, f32[96,2304]{1,0:T(8,128)}, f32[96,768]{1,0:T(8,128)}) custom-call(bf16[128,768]{1,0:T(8,128)(2,1)} %get-tuple-element.11.latent_hbm, bf16[32,8,384]{2,1,0:T(8,128)(2,1)} %get-tuple-element.12.gin_hbm, bf16[4,4,24,768]{3,2,1,0:T(8,128)(2,1)} %get-tuple-element.13.gmain_hbm), custom_call_target="tpu_custom_call" | custom-call | tf_op jit(solution)/shard_map/write_out/pallas_call | solution.py:691

commit v7 on v6

--- a/solution.py
+++ b/solution.py
@@ -564,10 +564,10 @@
             [(jf, jg.at[x * 8 + z], at_o(*f)) for f in others], jg.at[pl.ds(0, len(others))]
         )
         jg[x * 8 + z] = jf[...]
+        mo_cp.wait_recv()
+        l_main = load(0, mg, gmain_hbm)
         jg_cp.wait_recv()
         l_gin = load(9, jg, gin_hbm)
-        mo_cp.wait_recv()
-        l_main = load(0, mg, gmain_hbm)
         for cp in sent:
             cp.wait_send()
         l_latent.wait()

time: 91.5 us -> 91.2 us (level)
  no operation moved by 1% of the time
where the time goes in v7:
time: 91.2 us; the launch traced here: 91.1 us
  Pallas kernels  89.7 us (98%)
  between operations  1.47 us (2%)
    pallas_call x1, Pallas kernels, per_device(): pl.pallas_call(kernel, name='encode', out_shape=(jax.ShapeDtypeStruct((ow...  87.3 us
    pallas_call x1, Pallas kernels, per_device(): pl.pallas_call(write_out, name='write_out', out_shape=(jax.ShapeDtypeStru...  2.39 us

profile of v7, /device:TPU:1, one launch (start us, length us, event | category | flops | bytes accessed | tf_op | source)
XLA Modules:
  0.0 91.1 jit_solution(15330119518606406131)
XLA Ops:
  1.3 87.3 %encode.1 = (bf16[128,768]{1,0:T(8,128)(2,1)}, bf16[32,8,384]{2,1,0:T(8,128)(2,1)}, bf16[4,4,24,768]{3,2,1,0:T(8,128)(2,1)}) custom-call(bf16[1369,1024]{1,0:T(8,128)(2,1)} %bitcast.4, s32[8,1369]{1,0:T(8,128)} %bitcast.6, s32[1]{0:T(128)S(6)} %copy.12.count_hbm, bf16[1024,768]{1,0:T(8,128)(2,1)} %in_hbm.1, f32[768]{0:T(1024)} %gain_hbm.1, ...), custom_call_target="tpu_custom_call" | custom-call | tf_op jit(solution)/shard_map/encode/pallas_call | solution.py:660
  88.6 2.4 %write_out.1 = (bf16[128,768]{1,0:T(8,128)(2,1)}, f32[128,768]{1,0:T(8,128)}, f32[96,2304]{1,0:T(8,128)}, f32[96,768]{1,0:T(8,128)}) custom-call(bf16[128,768]{1,0:T(8,128)(2,1)} %get-tuple-element.11.latent_hbm, bf16[32,8,384]{2,1,0:T(8,128)(2,1)} %get-tuple-element.12.gin_hbm, bf16[4,4,24,768]{3,2,1,0:T(8,128)(2,1)} %get-tuple-element.13.gmain_hbm), custom_call_target="tpu_custom_call" | custom-call | tf_op jit(solution)/shard_map/write_out/pallas_call | solution.py:691
